TPU v7x, 512 devices: a whole 4x8x8 slice. The times are simulated.
512 devices in a mesh: tile: 8 (over z), comp: 64 (over y, x, core).
Axes of the slice: x: 4, y: 8, z: 8, core: 2. Of those that a mesh axis runs over, the one named last changes fastest.
Arguments:
- spectrum: float32 [1152, 8, 8192], P('comp', 'tile'), may hold values from 0.05 to 2
- sea_mask: int32 [512, 256], P('tile'), may hold values from 0 to 1, as said below
- sea_order: int32 [8, 8192], P('tile'), may hold values from 0 to 16383, as said below
- depth_class: int32 [512, 256], P('tile'), may hold values from 0 to 7
- wind_speed: float32 [512, 256], P('tile'), may hold values from 2 to 20
- wind_angle: float32 [512, 256], P('tile'), may hold values from -3.140625 to 3.140625
- speed_table: float32 [8, 36], replicated, may hold values from 0.2 to 0.7
- friction_table: float32 [8, 36], replicated, may hold values from 0.05 to 0.5
Outputs:
- spectrum_out: float32 [1152, 8, 8192], P('comp', 'tile')
Inputs may be any that keep to these rules, and one draw needn't show every extreme that they name: `sea_mask`: each grid row of a tile holds at most 128 sea cells and at least 64; in some tile every row holds exactly 128. `sea_order`: slots r * (128) to (r + 1) * 128 - 1 of a tile hold distinct cells of its local row r; that row's sea cells all appear there, before any land cell.
All inputs are finite; a program needn't handle non-finite values.
Results may differ from a plain program's by a relative error of at most 0.00009.
Values sent between devices are 32-bit elements; how exact they have to be, the bound alone decides.
A program may use at most 64 MiB of HBM per device.

v0:
```python
import math

import jax
import jax.numpy as jnp
from jax import lax
from jax.sharding import PartitionSpec as P

NF = 36
ND = 32


def from_behind(x, axis, by):
    count = lax.axis_size(axis)
    pairs = [(i, i + by) for i in range(count) if 0 <= i + by < count]
    return lax.ppermute(x, axis, pairs)


def wave_constants():
    theta = (jnp.arange(ND).astype(jnp.float32) + 0.5) * (2.0 * math.pi / ND)
    freq = 0.04 * jnp.exp(jnp.arange(NF).astype(jnp.float32) * (math.log(28.0) / (NF - 1)))
    return (theta, freq)


def component_tables(comp_ids, freq, depth_onehot, friction_table):
    freq_ids = comp_ids // ND
    dir_ids = comp_ids % ND
    pick = (freq_ids[:, None] == jnp.arange(NF, dtype=jnp.int32)[None, :]).astype(jnp.float32)
    comp_theta = (dir_ids.astype(jnp.float32) + 0.5) * (2.0 * math.pi / ND)
    comp_freq = jnp.dot(pick, freq, precision=lax.Precision.HIGHEST)
    friction_comp = jnp.dot(pick, friction_table.T, precision=lax.Precision.HIGHEST)
    friction = jnp.dot(friction_comp, depth_onehot, precision=lax.Precision.HIGHEST)
    return (pick, comp_theta, comp_freq, friction)


def point_factors(first_moment, second_moment, water_slot):
    safe = jnp.where(water_slot > 0, first_moment, 1.0)
    mean_freq = jnp.where(water_slot > 0, second_moment / safe, 1.0)
    steep = first_moment * mean_freq**4
    return (mean_freq, steep)


def partial_moments(energy, comp_freq):
    weight = 0.1 * comp_freq * (2.0 * math.pi / ND)
    weight_freq = weight * comp_freq
    return (
        jnp.sum(energy * weight[:, None], axis=0),
        jnp.sum(energy * weight_freq[:, None], axis=0),
    )


def apply_sources(
    energy, comp_freq, comp_theta, friction, wind_slot, angle_slot, water_slot, mean_freq, steep
):
    push = 0.05 * jnp.maximum(
        wind_slot[None, :] * comp_freq[:, None] * jnp.cos(comp_theta[:, None] - angle_slot[None, :])
        - 1.0,
        0.0,
    )
    damp = 2.0 * (comp_freq[:, None] / mean_freq[None, :]) * (steep * steep)[None, :]
    return water_slot[None, :] * energy * jnp.exp(push - damp - friction)


def body(
    spectrum, sea_mask, sea_order, depth_class, wind_speed, wind_angle, speed_table, friction_table
):
    theta, freq = wave_constants()
    local_comps = spectrum.shape[0]
    slot_count = spectrum.shape[2]
    rows = sea_mask.shape[0]
    columns = sea_mask.shape[1]
    row_slots = slot_count // rows
    depth_count = speed_table.shape[0]
    comp_count = lax.axis_size("comp")
    comp_ids = lax.axis_index("comp") * local_comps + jnp.arange(local_comps, dtype=jnp.int32)
    water_grid = sea_mask.astype(jnp.float32)
    water_cells = water_grid.reshape(-1)
    depth_flat = depth_class.reshape(-1)
    depth_onehot = (
        jnp.arange(depth_count, dtype=jnp.int32)[:, None] == depth_flat[None, :]
    ).astype(jnp.float32)
    row_start = (jnp.arange(rows, dtype=jnp.int32) * columns)[:, None]
    slot_column = sea_order[0].reshape(rows, row_slots) - row_start
    select = (
        slot_column[:, :, None] == jnp.arange(columns, dtype=jnp.int32)[None, None, :]
    ).astype(jnp.float32)
    cell_data = jnp.concatenate(
        [
            water_grid[None],
            wind_speed[None],
            wind_angle[None],
            depth_onehot.reshape(depth_count, rows, columns),
        ],
        axis=0,
    )
    slot_data = jnp.einsum(
        "arc,rjc->arj", cell_data, select, precision=lax.Precision.HIGHEST
    ).reshape(3 + depth_count, slot_count)
    water_slot = slot_data[0]
    wind_slot = slot_data[1]
    angle_slot = slot_data[2]
    slot_onehot = slot_data[3:]
    pick, comp_theta, comp_freq, friction_local = component_tables(
        comp_ids, freq, slot_onehot, friction_table
    )
    speed_comp = jnp.dot(pick, speed_table.T, precision=lax.Precision.HIGHEST)
    speed_cells = jnp.dot(speed_comp, depth_onehot, precision=lax.Precision.HIGHEST)
    energy_rows = spectrum[:, 0, :].reshape(local_comps, rows, row_slots)
    field = jnp.einsum("krj,rjc->krc", energy_rows, select, precision=lax.Precision.HIGHEST)
    field = field * water_grid[None]
    speed_water = (speed_cells * water_cells[None, :]).reshape(local_comps, rows, columns)
    along_x = jnp.cos(comp_theta)[:, None, None] * speed_water
    along_y = jnp.sin(comp_theta)[:, None, None] * speed_water
    plus_x = jnp.maximum(along_x, 0.0) * field
    minus_x = jnp.minimum(along_x, 0.0) * field
    plus_y = jnp.maximum(along_y, 0.0) * field
    minus_y = jnp.minimum(along_y, 0.0) * field
    lower_row = from_behind(plus_x[:, -1:, :], "tile", 1)
    upper_row = from_behind(minus_x[:, :1, :], "tile", -1)
    from_low_x = jnp.concatenate([lower_row, plus_x[:, :-1, :]], axis=1)
    from_high_x = jnp.concatenate([minus_x[:, 1:, :], upper_row], axis=1)
    from_low_y = jnp.pad(plus_y, ((0, 0), (0, 0), (1, 0)))[:, :, :-1]
    from_high_y = jnp.pad(minus_y, ((0, 0), (0, 0), (0, 1)))[:, :, 1:]
    outflow = (jnp.abs(along_x) + jnp.abs(along_y)) * field
    moved = field - outflow + from_low_x - from_high_x + from_low_y - from_high_y
    moved = moved * water_grid[None]
    moved_slots = jnp.einsum(
        "krc,rjc->krj", moved, select, precision=lax.Precision.HIGHEST
    ).reshape(local_comps, slot_count)
    gathered = lax.all_to_all(moved_slots, "comp", split_axis=1, concat_axis=0, tiled=True)
    share = slot_count // comp_count
    start = lax.axis_index("comp") * share
    all_ids = jnp.arange(local_comps * comp_count, dtype=jnp.int32)
    share_onehot = lax.dynamic_slice_in_dim(slot_onehot, start, share, 1)
    unused, all_theta, all_freq, friction_all = component_tables(
        all_ids, freq, share_onehot, friction_table
    )
    water_share = lax.dynamic_slice_in_dim(water_slot, start, share)
    first_moment, second_moment = partial_moments(gathered, all_freq)
    mean_freq, steep = point_factors(first_moment, second_moment, water_share)
    updated = apply_sources(
        gathered,
        all_freq,
        all_theta,
        friction_all,
        lax.dynamic_slice_in_dim(wind_slot, start, share),
        lax.dynamic_slice_in_dim(angle_slot, start, share),
        water_share,
        mean_freq,
        steep,
    )
    result = lax.all_to_all(updated, "comp", split_axis=0, concat_axis=1, tiled=True)
    return result.reshape(local_comps, 1, slot_count)


def solution(mesh):
    return jax.shard_map(
        body,
        mesh=mesh,
        in_specs=(
            P("comp", "tile", None),
            P("tile", None),
            P("tile", None),
            P("tile", None),
            P("tile", None),
            P("tile", None),
            P(),
            P(),
        ),
        out_specs=P("comp", "tile", None),
        check_vma=False,
    )
```

profile of v0, /device:TPU:1, one launch (start us, length us, event | category | flops | bytes accessed | tf_op | source)
XLA Modules:
  0.0 108.3 jit_solution(4400929329894325126)
XLA Ops:
  0.0 0.1 fusion.81
  0.1 0.9 fusion.90
  1.1 0.9 copy.19
  1.9 0.9 fusion.59
  2.8 0.8 convolution_multiply_fusion
  3.7 0.5 copy.21
  4.2 0.0 copy-start.6
  4.2 0.1 slice.55
  4.3 0.6 copy-done.6
  4.9 0.1 broadcast_subtract_fusion
  5.0 0.0 copy-done.8
  5.0 0.0 copy-start.1
  5.0 0.0 copy-start.10
  5.0 0.0 copy-start.4
  5.1 0.0 copy-start.5
  5.1 5.3 %fusion.18 = (f32[18,64,256]{2,0,1:T(8,128)S(1)}, f32[18,64,256]{2,0,1:T(8,128)S(1)}, f32[18,64,256]{2,0,1:T(8,128)S(1)}, f32[18,64,256]{2,0,1:T(8,128)}, f32[64,256,18]{1,2,0:T(8,128)}) fusion(f32[18,64,256]{2,1,0:T(8,128)S(1)} %slice.55, f32[18]{0:T(128)S(1)} %get-tuple-element.25, f32[18]{0:T(128)S(1)} %get-tuple-element.24, ...), kind=kOutput, calls=%fused_computation.26 | convolution fusion | flops 458326016 | bytes 7766160 | tf_op jit(solution)/shard_map/krj,rjc->krc/dot_general | solution.py:108
  10.4 0.6 slice.48
  11.0 5.4 %collective-permute-start = (f32[18,1,256]{2,0,1:T(8,128)}, f32[18,1,256]{2,0,1:T(8,128)}, u32[]{:S(2)}, u32[]{:S(2)}) collective-permute-start(f32[18,1,256]{2,0,1:T(8,128)} %slice.48), channel_id=1, source_target_pairs={{0,64},{64,128},{128,192},{192,256},{256,320},{320,384},{384,448},... | collective-permute-start | bytes 55304 | tf_op jit(solution)/shard_map/ppermute | solution.py:15
  16.4 0.6 slice.51
  17.0 1.3 %collective-permute-start.1 = (f32[18,1,256]{2,0,1:T(8,128)}, f32[18,1,256]{2,0,1:T(8,128)}, u32[]{:S(2)}, u32[]{:S(2)}) collective-permute-start(f32[18,1,256]{2,0,1:T(8,128)} %slice.51), channel_id=1, source_target_pairs={{64,0},{128,64},{192,128},{256,192},{320,256},{384,320},{448,384},... | collective-permute-start | bytes 55304 | tf_op jit(solution)/shard_map/ppermute | solution.py:15
  18.3 0.0 copy-done.1
  18.4 0.5 convolution_reduce_fusion
  19.0 1.1 %fusion.50 = f32[1152,8]{0,1:T(8,128)} fusion(f32[8,36]{1,0:T(8,128)S(1)} %copy-done.10, s32[1152]{0:T(1024)S(1)} %add_select_fusion), kind=kOutput, calls=%fused_computation.59 | convolution fusion | flops 4022784 | bytes 42624 | tf_op jit(solution)/shard_map/dot_general | solution.py:30
  20.1 0.0 copy-done.5
  20.2 5.4 %fusion.37 = f32[11,64,128]{2,0,1:T(8,128)S(1)} fusion(s32[64,128]{1,0:T(8,128)S(1)} %broadcast_subtract_fusion, f32[8,64,256]{2,0,1:T(8,128)S(1)} %fusion.51, f32[1,64,256]{2,0,1:T(1,128)S(1)} %broadcast_in_dim.12, f32[1,64,256]{2,0,1:T(1,128)S(1)} %broadcast_in_dim.11, f32[1,64,256]{2,0,1:T(1,128)S(1)} %broadcast_in_dim.10), kind=kOutput, calls=%fused_computation.41 | convolution fusion | flops 279461888 | bytes 1114112 | tf_op jit(solution)/shard_map/arc,rjc->arj/dot_general | solution.py:95
  25.6 0.8 fusion.89
  26.4 0.6 fusion.64
  27.0 1.2 %slice.49 = f32[18,63,256]{2,0,1:T(8,128)} slice(f32[18,64,256]{2,0,1:T(8,128)S(1)} %get-tuple-element.11), slice={[0:18], [0:63], [0:256]} | slice | bytes 2322432 | tf_op jit(solution)/shard_map/slice | solution.py:119
  28.2 1.3 %slice.50 = f32[18,63,256]{2,0,1:T(8,128)} slice(f32[18,64,256]{2,0,1:T(8,128)S(1)} %get-tuple-element.10), slice={[0:18], [1:64], [0:256]} | slice | bytes 2322432 | tf_op jit(solution)/shard_map/slice | solution.py:120
  29.5 0.1 mul.234
  29.6 0.1 mul.237
  29.8 1.3 %dynamic_slice.14 = f32[128]{0:T(128)} dynamic-slice(f32[8192]{0:T(1024)} %bitcast.53, s32[]{:T(128)S(6)} %select_n.57), dynamic_slice_sizes={128} | dynamic-slice | bytes 1028 | tf_op jit(solution)/shard_map/dynamic_slice | solution.py:146
  31.0 1.3 %dynamic_slice.13 = f32[128]{0:T(128)} dynamic-slice(f32[8192]{0:T(1024)} %bitcast.52, s32[]{:T(128)S(6)} %select_n.57), dynamic_slice_sizes={128} | dynamic-slice | bytes 1028 | tf_op jit(solution)/shard_map/dynamic_slice | solution.py:145
  32.4 0.0 collective-permute-done
  32.4 0.0 collective-permute-done.1
  32.4 8.1 %fusion.34 = f32[18,64,128]{2,0,1:T(8,128)} fusion(f32[18,64,256]{2,0,1:T(8,128)S(1)} %get-tuple-element.14, f32[18,64,256]{2,0,1:T(8,128)} %get-tuple-element.15, f32[18,64,256]{2,1,0:T(8,128)S(1)} %slice.55, f32[18,63,256]{2,0,1:T(8,128)} %slice.49, f32[18,1,256]{2,0,1:T(8,128)} %collective-permute-done, f32[18,1,256]{2,0,1:T(8,128)} %collective-permute-done.1, ...), kind=kOutput, calls=%fused_computation.40 | convolution fusion | flops 459210752 | bytes 7766160 | tf_op jit(solution)/shard_map/krc,rjc->krj/dot_general | solution.py:126
  40.5 11.2 %all-to-all-start = ((f32[18,64,128]{2,0,1:T(8,128)}), f32[18,64,128]{2,0,1:T(8,128)S(1)}, u32[]{:S(2)}, u32[]{:S(2)}) async-start(f32[18,64,128]{2,0,1:T(8,128)} %fusion.34), calls=%async_computation | async-start | bytes 1572864 | tf_op jit(solution)/shard_map/all_to_all | solution.py:129
  51.8 22.9 %all-to-all-done = f32[18,64,128]{2,0,1:T(8,128)S(1)} async-done(((f32[18,64,128]{2,0,1:T(8,128)}), f32[18,64,128]{2,0,1:T(8,128)S(1)}, u32[]{:S(2)}, u32[]{:S(2)}) %all-to-all-start) | async-done | bytes 589856 | tf_op jit(solution)/shard_map/all_to_all | solution.py:129
  74.7 0.1 all_to_all.26
  74.7 0.5 multiply_reduce_fusion.1
  75.2 0.1 multiply_multiply_fusion
  75.3 0.0 copy-done.11
  75.3 0.0 copy-done.12
  75.3 0.0 copy-done.13
  75.4 3.2 %fusion.7 = f32[1152,128]{1,0:T(8,128)S(1)} fusion(f32[1152,8]{0,1:T(8,128)S(1)} %copy-done.13, f32[1152,128]{1,0:T(8,128)S(1)} %all_to_all.26, f32[128]{0:T(128)S(1)} %get-tuple-element.7, f32[128]{0:T(128)S(1)} %get-tuple-element.8, f32[128]{0:T(128)S(1)} %copy-done.11, f32[1152]{0:T(1024)S(1)} %copy-done.7, f32[1152]{0:T(1024)S(1)} %convolution_reduce_fusion, ...), kind=kOutput, calls=%fused_computation.10 | convolution fusion | flops 15925248 | bytes 1239556 | tf_op jit(solution)/shard_map/dot_general | solution.py:31
  78.6 0.1 all_to_all.27
  78.6 28.7 %all_to_all.32 = f32[64,18,128]{2,1,0:T(8,128)S(1)} all-to-all(f32[64,18,128]{2,1,0:T(8,128)S(1)} %all_to_all.27), channel_id=1, replica_groups=mesh['tile'=8,'comp'=64] {'comp'}, dimensions={0} | all-to-all | bytes 1179648 | tf_op jit(solution)/shard_map/all_to_all | solution.py:151
  107.3 0.9 copy.17
  (26 shorter events, 0.3 us)
Async XLA Ops:
  0.0 5.0 %copy-start = (f32[18,1,8192]{2,1,0:T(1,128)S(1)}, f32[18,1,8192]{2,1,0:T(1,128)}, u32[]{:S(2)}) copy-start(f32[18,1,8192]{2,1,0:T(1,128)} %param.8) | copy-start | bytes 1769476
  0.1 4.9 %copy-start.8 = (f32[18]{0:T(128)}, f32[18]{0:T(128)S(1)}, u32[]{:S(2)}) copy-start(f32[18]{0:T(128)S(1)} %get-tuple-element.24) | copy-start | bytes 220
  0.1 4.9 %copy-start.9 = (f32[18]{0:T(128)}, f32[18]{0:T(128)S(1)}, u32[]{:S(2)}) copy-start(f32[18]{0:T(128)S(1)} %get-tuple-element.25) | copy-start | bytes 220
  4.2 0.8 copy-start.6
  5.0 13.3 %copy-start.1 = (s32[64,256]{1,0:T(8,128)S(1)}, s32[64,256]{1,0:T(8,128)}, u32[]{:S(2)}) copy-start(s32[64,256]{1,0:T(8,128)} %param.11) | copy-start | bytes 196612
  5.0 13.9 %copy-start.10 = (f32[8,36]{1,0:T(8,128)S(1)}, f32[8,36]{1,0:T(8,128)}, u32[]{:S(2)}) copy-start(f32[8,36]{1,0:T(8,128)} %param.15) | copy-start | bytes 3460
  5.0 15.0 %copy-start.4 = (f32[64,256]{1,0:T(8,128)S(1)}, f32[64,256]{1,0:T(8,128)}, u32[]{:S(2)}) copy-start(f32[64,256]{1,0:T(8,128)} %param.13) | copy-start | bytes 196612
  5.1 15.1 %copy-start.5 = (f32[64,256]{1,0:T(8,128)S(1)}, f32[64,256]{1,0:T(8,128)}, u32[]{:S(2)}) copy-start(f32[64,256]{1,0:T(8,128)} %param.12) | copy-start | bytes 196612
  11.0 21.4 %collective-permute-start = (f32[18,1,256]{2,0,1:T(8,128)}, f32[18,1,256]{2,0,1:T(8,128)}, u32[]{:S(2)}, u32[]{:S(2)}) collective-permute-start(f32[18,1,256]{2,0,1:T(8,128)} %slice.48), channel_id=1, source_target_pairs={{0,64},{64,128},{128,192},{192,256},{256,320},{320,384},{384,448},... | collective-permute-start | bytes 55304 | tf_op jit(solution)/shard_map/ppermute | solution.py:15
  17.0 15.4 %collective-permute-start.1 = (f32[18,1,256]{2,0,1:T(8,128)}, f32[18,1,256]{2,0,1:T(8,128)}, u32[]{:S(2)}, u32[]{:S(2)}) collective-permute-start(f32[18,1,256]{2,0,1:T(8,128)} %slice.51), channel_id=1, source_target_pairs={{64,0},{128,64},{192,128},{256,192},{320,256},{384,320},{448,384},... | collective-permute-start | bytes 55304 | tf_op jit(solution)/shard_map/ppermute | solution.py:15
  25.6 2.6 %copy-start.2 = (f32[11,64,128]{2,0,1:T(8,128)}, f32[11,64,128]{2,0,1:T(8,128)S(1)}, u32[]{:S(2)}) copy-start(f32[11,64,128]{2,0,1:T(8,128)S(1)} %fusion.37) | copy-start | bytes 1081348
  40.5 11.2 %copy-start.3 = (f32[11,64,128]{2,0,1:T(8,128)S(1)}, f32[11,64,128]{2,0,1:T(8,128)}, u32[]{:S(2)}) copy-start(f32[11,64,128]{2,0,1:T(8,128)} %copy-done.2) | copy-start | bytes 1081348
  40.5 34.2 %all-to-all-start = ((f32[18,64,128]{2,0,1:T(8,128)}), f32[18,64,128]{2,0,1:T(8,128)S(1)}, u32[]{:S(2)}, u32[]{:S(2)}) async-start(f32[18,64,128]{2,0,1:T(8,128)} %fusion.34), calls=%async_computation | async-start | bytes 1572864 | tf_op jit(solution)/shard_map/all_to_all | solution.py:129
  51.7 23.6 %copy-start.7 = (f32[1152]{0:T(1024)S(1)}, f32[1152]{0:T(1024)}, u32[]{:S(2)}) copy-start(f32[1152]{0:T(1024)} %fusion.64) | copy-start | bytes 13828
  51.7 23.6 %copy-start.11 = (f32[128]{0:T(128)S(1)}, f32[128]{0:T(128)}, u32[]{:S(2)}) copy-start(f32[128]{0:T(128)} %dynamic_slice.14) | copy-start | bytes 1540
  51.7 23.6 %copy-start.12 = (f32[128]{0:T(128)S(1)}, f32[128]{0:T(128)}, u32[]{:S(2)}) copy-start(f32[128]{0:T(128)} %dynamic_slice.13) | copy-start | bytes 1540
  51.7 23.6 %copy-start.13 = (f32[1152,8]{0,1:T(8,128)S(1)}, f32[1152,8]{0,1:T(8,128)}, u32[]{:S(2)}) copy-start(f32[1152,8]{0,1:T(8,128)} %fusion.50) | copy-start | bytes 110596
where the time goes:
time: 109 us; the launch traced here: 108 us
  blocking collectives  28.7 us (26%)
  matrix products  25.4 us (23%)
  waiting for transfers between devices  22.9 us (21%)
  starting transfers between devices  17.9 us (16%)
  local copies, waits for them, and re-layouts  10.8 us (10%)
  other arithmetic  2.29 us (2%)
    all_to_all x1, blocking collectives, body(): lax.all_to_all(updated, 'comp', split_axis=0, concat_axis=1, tiled=True)  28.7 us
    all_to_all x1, waiting for transfers between devices, body(): lax.all_to_all(moved_slots, 'comp', split_axis=1, concat_axis=0, tiled=True)  22.9 us
    all_to_all x1, starting transfers between devices, body(): lax.all_to_all(moved_slots, 'comp', split_axis=1, concat_axis=0, tiled=True)  11.2 us
    dot_general x1, matrix products, body(): jnp.einsum('krc,rjc->krj', moved, select, precision=lax.Precision.HIGHEST)  8.09 us
    ppermute x2, starting transfers between devices, from_behind(): return lax.ppermute(x, axis, pairs)  6.68 us
    dot_general x1, matrix products, body(): jnp.einsum('arc,rjc->arj', cell_data, select, precision=lax.Precision.HIG...  5.4 us
    dot_general x1, matrix products, body(): jnp.einsum('krj,rjc->krc', energy_rows, select, precision=lax.Precision.H...  5.31 us
    dot_general x1, matrix products, component_tables(): jnp.dot(friction_comp, depth_onehot, precision=lax.Precision.HIGHEST)  3.21 us
  transfers between devices with their start and end apart: 3, of which 1 were waited for; matrix products, arithmetic and copies ran while one was open for 14% of the time, Pallas kernels for 0%

commit v1 on v0

v1 whole, which is shorter than its diff:
```python
import functools
import math

import jax
import jax.numpy as jnp
import numpy as np
from jax import lax
from jax.experimental import pallas as pl
from jax.experimental.pallas import tpu as pltpu
from jax.sharding import PartitionSpec as P

NF = 36
ND = 32
LANES = 128
GROUP = 8
MESH = pl.DeviceIdType.MESH


def constants():
    theta = (np.arange(ND) + 0.5) * (2.0 * math.pi / ND)
    freq = 0.04 * np.exp(np.arange(NF) * (math.log(28.0) / (NF - 1)))
    weight = 0.1 * freq * (2.0 * math.pi / ND)
    return np.concatenate([np.cos(theta), np.sin(theta), freq, weight]).astype(np.float32)


def take(x, index):
    return jnp.take_along_axis(x, index, axis=1, mode="promise_in_bounds")


def take_wide(low, high, column):
    index = column & (LANES - 1)
    return jnp.where(column >= LANES, take(high, index), take(low, index))


def step_kernel(
    tiles, y_count,
    spectrum_hbm, order_hbm, mask_hbm, depth_hbm, wind_hbm, angle_hbm, speed_s, friction_s, const_s,
    p_ref, x_ref,
    e, order_v, mask_v, depth_v, wind_v, angle_v,
    col_v, water_v, inv, nbr, nbr_mask, spd, fri, wx, wy, g, edge, coef, halo_out, halo_in,
    part, part_in, total, total_in, damp_out, damp,
    in_sem, halo_send, halo_recv, a_send, a_recv, b_send, b_recv, c_send, c_recv,
):
    comps, rows, lanes = e.shape
    tile = lax.axis_index("tile")
    comp = lax.axis_index("comp")
    q = comp % GROUP
    y = comp // GROUP
    first = comp * comps
    f0 = first // ND
    f1 = (first + comps - 1) // ND
    after = (tile + 1) % tiles
    before = (tile + tiles - 1) % tiles

    copies = [
        pltpu.make_async_copy(src, dst, in_sem.at[i])
        for i, (src, dst) in enumerate(
            [(order_hbm, order_v), (mask_hbm, mask_v), (depth_hbm, depth_v), (spectrum_hbm, e),
             (wind_hbm, wind_v), (angle_hbm, angle_v)]
        )
    ]
    for copy in copies:
        copy.start()

    barrier = pltpu.get_barrier_semaphore()
    for o in range(1, GROUP):
        pl.semaphore_signal(barrier, inc=1, device_id=(tile, y * GROUP + (q + o) % GROUP), device_id_type=MESH)
    for o in range(1, y_count):
        pl.semaphore_signal(barrier, inc=1, device_id=(tile, (y + o) % y_count * GROUP + q), device_id_type=MESH)
    pl.semaphore_signal(barrier, inc=1, device_id=(after, comp), device_id_type=MESH)
    pl.semaphore_signal(barrier, inc=1, device_id=(before, comp), device_id_type=MESH)

    zero8 = jnp.zeros((8, lanes), jnp.float32)
    for k in range(comps):
        g[k, 0:8, :] = zero8
        g[k, rows + 8 : rows + 16, :] = zero8
    none8 = jnp.full((8, lanes), -1, jnp.int32)
    for h in range(2):
        inv[h, 0:8, :] = none8
        inv[h, rows + 8 : rows + 16, :] = none8

    copies[0].wait()
    copies[1].wait()
    lane = lax.broadcasted_iota(jnp.int32, (rows, lanes), 1)
    row = lax.broadcasted_iota(jnp.int32, (rows, lanes), 0)
    column = order_v[...] - row * (2 * lanes)
    col_v[...] = column
    water = take_wide(mask_v[:, :lanes], mask_v[:, lanes:], column)
    water_v[...] = water.astype(jnp.float32)
    wet = jnp.where(water > 0, column, 4 * lanes)
    inv[0, 8 : rows + 8, :] = wet
    unroll = 8

    def invert(i, carry):
        low, high = carry
        base = pltpu.roll(inv[0, 8 : rows + 8, :], i * unroll, 1)
        for j in range(unroll):
            turned = base if j == 0 else pltpu.roll(base, j, 1)
            slot = (lane - (i * unroll + j)) & (lanes - 1)
            low = jnp.where(turned == lane, slot, low)
            high = jnp.where(turned == lane + lanes, slot, high)
        return low, high

    none = jnp.full((rows, lanes), -1, jnp.int32)
    low, high = lax.fori_loop(0, lanes // unroll, invert, (none, none))
    inv[0, 8 : rows + 8, :] = low
    inv[1, 8 : rows + 8, :] = high

    water = water_v[...]

    def neighbour(where, found, valid):
        nbr[where] = jnp.maximum(found, 0)
        nbr_mask[where] = jnp.where(valid, water, 0.0)

    for b in range(2):
        found = take_wide(inv[0, 7 + 2 * b : 7 + 2 * b + rows, :], inv[1, 7 + 2 * b : 7 + 2 * b + rows, :], column)
        neighbour(b, found, found >= 0)
        shifted = column - 1 + 2 * b
        inside = (shifted >= 0) & (shifted < 2 * lanes)
        found = take_wide(low, high, shifted & (2 * lanes - 1))
        neighbour(2 + b, found, (found >= 0) & inside)

    copies[2].wait()
    depth = take_wide(depth_v[:, :lanes], depth_v[:, lanes:], column)
    for i, f in enumerate((f0, f1)):
        s = jnp.full((rows, lanes), speed_s[0, f])
        r = jnp.full((rows, lanes), friction_s[0, f])
        for n in range(1, 8):
            s = jnp.where(depth == n, speed_s[n, f], s)
            r = jnp.where(depth == n, friction_s[n, f], r)
        spd[i] = s * water
        fri[i] = r

    coef[...] = jnp.zeros_like(coef)
    copies[3].wait()

    def advect(k, carry):
        m0, m1 = carry
        f = (first + k) // ND
        d = (first + k) % ND
        i = f - f0
        bx = (d + 8) // 16 % 2
        by = d // 16
        cos = jnp.abs(const_s[d])
        sin = jnp.abs(const_s[ND + d])
        weight = const_s[2 * ND + NF + f]
        energy = e[k]
        flux = energy * spd[i]
        g[k, 8 : rows + 8, :] = flux
        gx = take(g[k, pl.ds(7 + 2 * bx, rows), :], nbr[bx])
        gy = take(flux, nbr[2 + by])
        moved = energy * water_v[...] - (cos + sin) * flux + cos * (nbr_mask[bx] * gx) + sin * (nbr_mask[2 + by] * gy)
        p_ref[k] = moved
        edge[0, pl.ds(k, 1), :] = flux[rows - 1 : rows]
        edge[1, pl.ds(k, 1), :] = flux[0:1]
        coef[bx * 2 + i, pl.ds(k, 1), :] = jnp.full((1, lanes), cos)
        return m0 + weight * moved, m1 + (weight * const_s[2 * ND + f]) * moved

    zero = jnp.zeros((rows, lanes), jnp.float32)
    m0, m1 = lax.fori_loop(0, comps, advect, (zero, zero))
    for n in range(GROUP):
        part[n, 0] = m0[8 * n : 8 * n + 8]
        part[n, 1] = m1[8 * n : 8 * n + 8]

    pad = edge.shape[1]
    for b, at in ((0, rows - 1), (1, 0)):
        for h in range(2):
            found = jnp.broadcast_to(inv[h, 8 + at : 9 + at, :], (pad, lanes))
            halo_out[b, h] = jnp.where(found >= 0, take(edge[b], jnp.maximum(found, 0)), 0.0)

    pl.semaphore_wait(barrier, GROUP - 1 + y_count - 1 + 2)

    halos = [
        pltpu.make_async_remote_copy(
            src_ref=halo_out.at[b], dst_ref=halo_in.at[b], send_sem=halo_send.at[b], recv_sem=halo_recv.at[b],
            device_id=(to, comp), device_id_type=MESH,
        )
        for b, to in ((0, after), (1, before))
    ]
    for copy in halos:
        copy.start()

    def scatter(n):
        return pltpu.make_async_remote_copy(
            src_ref=part.at[n], dst_ref=part_in.at[q], send_sem=a_send.at[n], recv_sem=a_recv.at[q],
            device_id=(tile, y * GROUP + n), device_id_type=MESH,
        )

    def send_part(n):
        @pl.when(q != n)
        def _():
            scatter(n).start()

    for n in range(1, GROUP - 1):
        send_part(n)

    copies[4].wait()
    copies[5].wait()
    wind = take_wide(wind_v[:, :lanes], wind_v[:, lanes:], column)
    angle = take_wide(angle_v[:, :lanes], angle_v[:, lanes:], column)
    wx[...] = 0.05 * wind * jnp.cos(angle)
    wy[...] = 0.05 * wind * jnp.sin(angle)

    for copy in halos:
        copy.wait()
    sub = lax.broadcasted_iota(jnp.int32, (8, lanes), 0)
    live = (
        ((tile + tiles - 1) // tiles).astype(jnp.float32),
        ((2 * tiles - 2 - tile) // tiles).astype(jnp.float32),
    )
    for b, at in ((0, 0), (1, rows - 1)):
        column1 = jnp.broadcast_to(col_v[at : at + 1, :], (pad, lanes))
        scale = water_v[at : at + 1, :] * live[b]
        came = take_wide(halo_in[b, 0], halo_in[b, 1], column1) * scale
        c0 = came * coef[2 * b]
        c1 = came * coef[2 * b + 1]
        edge[b] = c0 + c1
        s0 = jnp.sum(c0[:comps], axis=0, keepdims=True)
        s1 = jnp.sum(c1[:comps], axis=0, keepdims=True)
        w0 = const_s[2 * ND + NF + f0]
        w1 = const_s[2 * ND + NF + f1]
        d0 = w0 * s0 + w1 * s1
        d1 = (w0 * const_s[2 * ND + f0]) * s0 + (w1 * const_s[2 * ND + f1]) * s1
        n = at // 8
        here = sub == at % 8
        part[n, 0] += jnp.where(here, d0, 0.0)
        part[n, 1] += jnp.where(here, d1, 0.0)
        send_part(n)

    def boundary(k, carry):
        d = (first + k) % ND
        bx = (d + 8) // 16 % 2
        p_ref[k, pl.ds((rows - 1) * bx, 1), :] += edge[bx, pl.ds(k, 1), :]
        return carry

    lax.fori_loop(0, comps, boundary, 0)

    def sources(k, carry):
        f = (first + k) // ND
        d = (first + k) % ND
        freq = const_s[2 * ND + f]
        push = jnp.maximum((freq * const_s[d]) * wx[...] + (freq * const_s[ND + d]) * wy[...] - 0.05, 0.0)
        p_ref[k] = p_ref[k] * jnp.exp(push - fri[f - f0])
        return carry

    lax.fori_loop(0, comps, sources, 0)

    a0 = part[q, 0]
    a1 = part[q, 1]
    for o in range(1, GROUP):
        source = (q + GROUP - o) % GROUP
        pltpu.make_async_remote_copy(
            src_ref=part.at[o], dst_ref=part_in.at[source], send_sem=a_send.at[o], recv_sem=a_recv.at[source],
            device_id=(tile, y * GROUP + (q + o) % GROUP), device_id_type=MESH,
        ).wait_recv()
        a0 += part_in[source, 0]
        a1 += part_in[source, 1]
    total[0] = a0
    total[1] = a1

    exchanges = [
        pltpu.make_async_remote_copy(
            src_ref=total, dst_ref=total_in.at[y], send_sem=b_send.at[o], recv_sem=b_recv.at[y],
            device_id=(tile, (y + o) % y_count * GROUP + q), device_id_type=MESH,
        )
        for o in range(1, y_count)
    ]
    for copy in exchanges:
        copy.start()
    for o in range(1, y_count):
        source = (y + y_count - o) % y_count
        pltpu.make_async_remote_copy(
            src_ref=total, dst_ref=total_in.at[source], send_sem=b_send.at[o], recv_sem=b_recv.at[source],
            device_id=(tile, (y + o) % y_count * GROUP + q), device_id_type=MESH,
        ).wait_recv()
        a0 += total_in[source, 0]
        a1 += total_in[source, 1]

    wet_here = water_v[pl.ds(pl.multiple_of(q * 8, 8), 8), :] > 0
    mean = jnp.where(wet_here, a1 / jnp.where(wet_here, a0, 1.0), 1.0)
    square = mean * mean
    alpha = a0 * (square * square)
    mine = 2.0 * alpha * alpha / mean
    damp_out[...] = mine
    gathers = [
        pltpu.make_async_remote_copy(
            src_ref=damp_out, dst_ref=damp.at[q], send_sem=c_send.at[o], recv_sem=c_recv.at[q],
            device_id=(tile, y * GROUP + (q + o) % GROUP), device_id_type=MESH,
        )
        for o in range(1, GROUP)
    ]
    for copy in gathers:
        copy.start()
    damp[q] = mine
    for o in range(1, GROUP):
        source = (q + GROUP - o) % GROUP
        pltpu.make_async_remote_copy(
            src_ref=damp_out, dst_ref=damp.at[source], send_sem=c_send.at[o], recv_sem=c_recv.at[source],
            device_id=(tile, y * GROUP + (q + o) % GROUP), device_id_type=MESH,
        ).wait_recv()
    factor = damp[...].reshape(rows, lanes)
    x_ref[0] = jnp.exp(-const_s[2 * ND + f0] * factor)
    x_ref[1] = jnp.exp(-const_s[2 * ND + f1] * factor)

    for n in range(GROUP):
        @pl.when(q != n)
        def _():
            scatter(n).wait_send()
    for copy in exchanges:
        copy.wait_send()
    for copy in gathers:
        copy.wait_send()


def body(tiles, y_count, spectrum, sea_mask, sea_order, depth_class, wind_speed, wind_angle, speed_table, friction_table):
    comps = spectrum.shape[0]
    rows = sea_mask.shape[0]
    f32, i32 = jnp.float32, jnp.int32
    hbm = pl.BlockSpec(memory_space=pltpu.HBM)
    vmem = pl.BlockSpec(memory_space=pltpu.VMEM)
    smem = pl.BlockSpec(memory_space=pltpu.SMEM)
    grid = (rows, LANES)
    wide = (rows, 2 * LANES)
    pad = -(-comps // 8) * 8
    V, D = pltpu.VMEM, pltpu.SemaphoreType.DMA
    p, x = pl.pallas_call(
        functools.partial(step_kernel, tiles, y_count),
        out_shape=(jax.ShapeDtypeStruct((comps,) + grid, f32), jax.ShapeDtypeStruct((2,) + grid, f32)),
        in_specs=[hbm] * 6 + [smem] * 3,
        out_specs=(vmem, vmem),
        scratch_shapes=[
            V((comps,) + grid, f32), V(grid, i32), V(wide, i32), V(wide, i32), V(wide, f32), V(wide, f32),
            V(grid, i32), V(grid, f32), V((2, rows + 16, LANES), i32), V((4,) + grid, i32), V((4,) + grid, f32),
            V((2,) + grid, f32), V((2,) + grid, f32), V(grid, f32), V(grid, f32),
            V((comps, rows + 16, LANES), f32), V((2, pad, LANES), f32), V((4, pad, LANES), f32),
            V((2, 2, pad, LANES), f32), V((2, 2, pad, LANES), f32),
            V((GROUP, 2, 8, LANES), f32), V((GROUP, 2, 8, LANES), f32),
            V((2, 8, LANES), f32), V((y_count, 2, 8, LANES), f32),
            V((8, LANES), f32), V((GROUP, 8, LANES), f32),
            D((6,)), D((2,)), D((2,)), D((GROUP,)), D((GROUP,)), D((y_count,)), D((y_count,)), D((GROUP,)), D((GROUP,)),
        ],
        compiler_params=pltpu.CompilerParams(collective_id=0, has_side_effects=True, vmem_limit_bytes=32 << 20),
        name="wave_step",
    )(
        spectrum.reshape(comps, rows, LANES), sea_order.reshape(grid), sea_mask, depth_class, wind_speed, wind_angle,
        speed_table, friction_table, jnp.asarray(constants()),
    )
    first = lax.axis_index("comp") * comps
    second = (first + jnp.arange(comps)) // ND > first // ND
    result = p * jnp.where(second[:, None, None], x[1][None], x[0][None])
    return result.reshape(spectrum.shape)


def solution(mesh):
    return jax.shard_map(
        functools.partial(body, mesh.shape["tile"], mesh.shape["comp"] // GROUP),
        mesh=mesh,
        in_specs=(
            P("comp", "tile", None),
            P("tile", None),
            P("tile", None),
            P("tile", None),
            P("tile", None),
            P("tile", None),
            P(),
            P(),
        ),
        out_specs=P("comp", "tile", None),
        check_vma=False,
    )
```

time: 109 us -> 41.3 us (0.38)
  Pallas kernels: 0 us -> 34.7 us
  blocking collectives: 28.7 us -> 0 us
  matrix products: 25.4 us -> 0 us
  waiting for transfers between devices: 22.9 us -> 0 us
  starting transfers between devices: 17.9 us -> 0 us
  local copies, waits for them, and re-layouts: 10.8 us -> 5.15 us
  other arithmetic: 2.29 us -> 0.95 us
    pallas_call x0 -> x1, Pallas kernels: none -> 34.7 us  [body(): pl.pallas_call(functools.partial(step_kernel, tiles, y_count), out_shape=...]
    all_to_all x1 -> x0, blocking collectives: 28.7 us -> none  [body(): lax.all_to_all(updated, 'comp', split_axis=0, concat_axis=1, tiled=True)]
    dot_general x8 -> x0, matrix products: 25.4 us -> none  [the longest x1 8.09 us: body(): jnp.einsum('krc,rjc->krj', moved, select, precision=lax.Precision.HIGHEST)]
    all_to_all x1 -> x0, waiting for transfers between devices: 22.9 us -> none  [body(): lax.all_to_all(moved_slots, 'comp', split_axis=1, concat_axis=0, tiled=True)]
    all_to_all x1 -> x0, starting transfers between devices: 11.2 us -> none  [body(): lax.all_to_all(moved_slots, 'comp', split_axis=1, concat_axis=0, tiled=True)]
    ppermute x2 -> x0, starting transfers between devices: 6.68 us -> none  [from_behind(): return lax.ppermute(x, axis, pairs)]
    slice x6 -> x0, local copies, waits for them, and re-layouts: 4.53 us -> none  [the longest x1 1.27 us: body(): from_high_x = jnp.concatenate([minus_x[:, 1:, :], upper_row], axis=1)]
    unnamed x31 -> x18, local copies, waits for them, and re-layouts: 2.13 us -> 5.15 us
  transfers between devices with their start and end apart: 3 -> 0, of which waited for: 1 -> 0; matrix products, arithmetic and copies ran while one was open for 14% -> 0% of each run, Pallas kernels for 0% -> 0%
where the time goes in v1:
time: 41.3 us; the launch traced here: 40.8 us
  Pallas kernels  34.7 us (84%)
  local copies, waits for them, and re-layouts  5.15 us (12%)
  other arithmetic  0.95 us (2%)
    pallas_call x1, Pallas kernels, body(): pl.pallas_call(functools.partial(step_kernel, tiles, y_count), out_shape=...  34.7 us
    unnamed x18, local copies, waits for them, and re-layouts  5.15 us
    mul x1, other arithmetic, body(): result = p * jnp.where(second[:, None, None], x[1][None], x[0][None])  0.94 us

profile of v1, /device:TPU:1, one launch (start us, length us, event | category | flops | bytes accessed | tf_op | source)
XLA Modules:
  0.0 40.8 jit_solution(8438821992012034077)
XLA Ops:
  0.0 0.0 copy-start.5
  0.0 0.0 copy-start.7
  0.0 0.0 copy-start.6
  0.0 0.0 copy-start.8
  0.0 0.7 %copy-done.5 = s32[1,8192]{1,0:T(1,128)S(1)} copy-done((s32[1,8192]{1,0:T(1,128)S(1)}, s32[1,8192]{1,0:T(1,128)}, u32[]{:S(2)}) %copy-start.5) | copy-done | bytes 32792
  0.8 0.0 copy-done.7
  0.8 0.0 copy-done.6
  0.8 0.0 copy-done.8
  0.8 0.0 copy-start
  0.8 1.1 %copy-done = f32[18,1,8192]{2,1,0:T(1,128)S(1)} copy-done((f32[18,1,8192]{2,1,0:T(1,128)S(1)}, f32[18,1,8192]{2,1,0:T(1,128)}, u32[]{:S(2)}) %copy-start) | copy-done | bytes 589848
  1.8 0.0 copy-start.1
  1.8 0.8 %copy-done.1 = s32[64,256]{1,0:T(8,128)S(1)} copy-done((s32[64,256]{1,0:T(8,128)S(1)}, s32[64,256]{1,0:T(8,128)}, u32[]{:S(2)}) %copy-start.1) | copy-done | bytes 65560
  2.7 0.0 copy-start.2
  2.7 0.8 %copy-done.2 = s32[64,256]{1,0:T(8,128)S(1)} copy-done((s32[64,256]{1,0:T(8,128)S(1)}, s32[64,256]{1,0:T(8,128)}, u32[]{:S(2)}) %copy-start.2) | copy-done | bytes 65560
  3.5 0.0 copy-start.3
  3.5 0.8 %copy-done.3 = f32[64,256]{1,0:T(8,128)S(1)} copy-done((f32[64,256]{1,0:T(8,128)S(1)}, f32[64,256]{1,0:T(8,128)}, u32[]{:S(2)}) %copy-start.3) | copy-done | bytes 65560
  4.4 0.0 copy-start.4
  4.4 0.8 %copy-done.4 = f32[64,256]{1,0:T(8,128)S(1)} copy-done((f32[64,256]{1,0:T(8,128)S(1)}, f32[64,256]{1,0:T(8,128)}, u32[]{:S(2)}) %copy-start.4) | copy-done | bytes 65560
  5.2 34.7 %wave_step.1 = (f32[18,64,128]{2,1,0:T(8,128)S(1)}, f32[2,64,128]{2,1,0:T(8,128)S(1)}) custom-call(f32[18,64,128]{2,1,0:T(8,128)S(1)} %bitcast.7, s32[64,128]{1,0:T(8,128)S(1)} %bitcast.8, s32[64,256]{1,0:T(8,128)S(1)} %copy-done.1, s32[64,256]{1,0:T(8,128)S(1)} %copy-done.2, f32[64,256]{1,0:T(8,128)S(1)} %copy-done.3, f32[64,256]{1,0:T(8,128)S(1)} %copy-done.4, ...), custom_call_target="tpu_custom_call" | custom-call | tf_op jit(solution)/shard_map/wave_step/pallas_call | solution.py:326
  39.9 0.9 %select_multiply_fusion = f32[18,64,128]{2,1,0:T(8,128)} fusion(f32[18,64,128]{2,1,0:T(8,128)S(1)} %get-tuple-element.7, f32[64,128]{1,0:T(8,128)S(1)} %get-tuple-element.10, f32[64,128]{1,0:T(8,128)S(1)} %get-tuple-element.9, pred[18]{0:T(512)(128)(4,1)S(1)} %fusion), kind=kLoop, calls=%fused_computation | loop fusion | flops 294912 | bytes 1245202 | tf_op jit(solution)/shard_map/mul | solution.py:350
  (2 shorter events, 0.0 us)
Async XLA Ops:
  0.0 0.8 %copy-start.5 = (s32[1,8192]{1,0:T(1,128)S(1)}, s32[1,8192]{1,0:T(1,128)}, u32[]{:S(2)}) copy-start(s32[1,8192]{1,0:T(1,128)} %param.11) | copy-start | bytes 98308
  0.0 0.8 %copy-start.7 = (f32[8,36]{1,0:T(8,128)S(1)}, f32[8,36]{1,0:T(8,128)}, u32[]{:S(2)}) copy-start(f32[8,36]{1,0:T(8,128)} %friction_s.1) | copy-start | bytes 3460
  0.0 0.8 %copy-start.6 = (f32[8,36]{1,0:T(8,128)S(1)}, f32[8,36]{1,0:T(8,128)}, u32[]{:S(2)}) copy-start(f32[8,36]{1,0:T(8,128)} %speed_s.1) | copy-start | bytes 3460
  0.0 0.7 %copy-start.8 = (f32[136]{0:T(256)S(1)}, f32[136]{0:T(256)}, u32[]{:S(2)}) copy-start(f32[136]{0:T(256)} %constant.33.clone.const_s) | copy-start | bytes 1636
  0.8 1.1 %copy-start = (f32[18,1,8192]{2,1,0:T(1,128)S(1)}, f32[18,1,8192]{2,1,0:T(1,128)}, u32[]{:S(2)}) copy-start(f32[18,1,8192]{2,1,0:T(1,128)} %param.9) | copy-start | bytes 1769476
  1.8 0.8 %copy-start.1 = (s32[64,256]{1,0:T(8,128)S(1)}, s32[64,256]{1,0:T(8,128)}, u32[]{:S(2)}) copy-start(s32[64,256]{1,0:T(8,128)} %mask_hbm.1) | copy-start | bytes 196612
  2.7 0.8 %copy-start.2 = (s32[64,256]{1,0:T(8,128)S(1)}, s32[64,256]{1,0:T(8,128)}, u32[]{:S(2)}) copy-start(s32[64,256]{1,0:T(8,128)} %depth_hbm.1) | copy-start | bytes 196612
  3.5 0.8 %copy-start.3 = (f32[64,256]{1,0:T(8,128)S(1)}, f32[64,256]{1,0:T(8,128)}, u32[]{:S(2)}) copy-start(f32[64,256]{1,0:T(8,128)} %wind_hbm.1) | copy-start | bytes 196612
  4.4 0.8 %copy-start.4 = (f32[64,256]{1,0:T(8,128)S(1)}, f32[64,256]{1,0:T(8,128)}, u32[]{:S(2)}) copy-start(f32[64,256]{1,0:T(8,128)} %angle_hbm.1) | copy-start | bytes 196612

commit v2 on v1

v2 whole, which is shorter than its diff:
```python
import functools
import math

import jax
import jax.numpy as jnp
import numpy as np
from jax import lax
from jax.experimental import pallas as pl
from jax.experimental.pallas import tpu as pltpu
from jax.sharding import PartitionSpec as P

NF = 36
ND = 32
LANES = 128
GROUP = 8
MESH = pl.DeviceIdType.MESH


def constants():
    theta = (np.arange(ND) + 0.5) * (2.0 * math.pi / ND)
    freq = 0.04 * np.exp(np.arange(NF) * (math.log(28.0) / (NF - 1)))
    weight = 0.1 * freq * (2.0 * math.pi / ND)
    return np.concatenate([np.cos(theta), np.sin(theta), freq, weight]).astype(np.float32)


def take(x, index):
    return jnp.take_along_axis(x, index, axis=1, mode="promise_in_bounds")


def take_wide(low, high, column):
    index = column & (LANES - 1)
    return jnp.where(column >= LANES, take(high, index), take(low, index))


def step_kernel(
    tiles, y_count,
    spectrum_hbm, order_hbm, mask_hbm, depth_hbm, wind_hbm, angle_hbm, speed_hbm, friction_hbm, const_hbm,
    p_ref, x_ref,
    speed_s, friction_s, const_s,
    e, order_v, mask_v, depth_v, wind_v, angle_v,
    col_v, water_v, inv, nbr, spd, sx, sy, fri, wx, wy, coef, halo_out, halo_in,
    part, part_in, total, total_in, damp_out, damp,
    in_sem, halo_send, halo_recv, a_send, a_recv, b_send, b_recv, c_send, c_recv,
):
    comps = e.shape[0]
    rows, lanes = order_v.shape
    tile = lax.axis_index("tile")
    comp = lax.axis_index("comp")
    q = comp % GROUP
    y = comp // GROUP
    first = comp * comps
    f0 = first // ND
    f1 = (first + comps - 1) // ND
    after = (tile + 1) % tiles
    before = (tile + tiles - 1) % tiles
    inner = slice(8, rows + 8)

    copies = [
        pltpu.make_async_copy(src, dst, in_sem.at[i])
        for i, (src, dst) in enumerate(
            [(order_hbm, order_v), (mask_hbm, mask_v), (depth_hbm, depth_v),
             (speed_hbm, speed_s), (friction_hbm, friction_s), (const_hbm, const_s),
             (spectrum_hbm, e.at[:, inner, :]), (wind_hbm, wind_v), (angle_hbm, angle_v)]
        )
    ]
    for copy in copies:
        copy.start()

    barrier = pltpu.get_barrier_semaphore()
    for o in range(1, y_count):
        pl.semaphore_signal(barrier, inc=1, device_id=(tile, (y + o) % y_count * GROUP + q), device_id_type=MESH)
    for o in range(1, GROUP):
        pl.semaphore_signal(barrier, inc=1, device_id=(tile, y * GROUP + (q + o) % GROUP), device_id_type=MESH)
    pl.semaphore_signal(barrier, inc=1, device_id=(after, comp), device_id_type=MESH)
    pl.semaphore_signal(barrier, inc=1, device_id=(before, comp), device_id_type=MESH)

    zero8 = jnp.zeros((8, lanes), jnp.float32)
    none8 = jnp.full((8, lanes), -1, jnp.int32)
    for pad in (slice(0, 8), slice(rows + 8, rows + 16)):
        for k in range(comps):
            e[k, pad, :] = zero8
        for h in range(2):
            inv[h, pad, :] = none8
            spd[h, pad, :] = zero8
    coef[...] = jnp.zeros_like(coef)

    for copy in copies[:5]:
        copy.wait()
    lane = lax.broadcasted_iota(jnp.int32, (rows, lanes), 1)
    row = lax.broadcasted_iota(jnp.int32, (rows, lanes), 0)
    column = order_v[...] - row * (2 * lanes)
    col_v[...] = column
    wet = take_wide(mask_v[:, :lanes], mask_v[:, lanes:], column) > 0
    water = jnp.where(wet, 1.0, 0.0)
    water_v[...] = water
    wet_column = jnp.where(wet, column, 4 * lanes)
    depth = take_wide(depth_v[:, :lanes], depth_v[:, lanes:], column)
    for i, f in enumerate((f0, f1)):
        s = jnp.full((rows, lanes), speed_s[0, f])
        r = jnp.full((rows, lanes), friction_s[0, f])
        for n in range(1, 8):
            s = jnp.where(depth == n, speed_s[n, f], s)
            r = jnp.where(depth == n, friction_s[n, f], r)
        spd[i, inner, :] = s * water
        fri[i] = r

    copies[5].wait()
    copies[6].wait()
    for b, at in ((0, rows - 1), (1, 0)):
        for k in range(comps):
            i = (first + k) // ND - f0
            halo_out[b, k : k + 1, :] = e[k, 8 + at : 9 + at, :] * spd[i, 8 + at : 9 + at, :]
        halo_out[b, comps : comps + 1, :] = wet_column[at : at + 1].astype(jnp.float32)

    pl.semaphore_wait(barrier, GROUP - 1 + y_count - 1 + 2)
    halos = [
        pltpu.make_async_remote_copy(
            src_ref=halo_out.at[b], dst_ref=halo_in.at[b], send_sem=halo_send.at[b], recv_sem=halo_recv.at[b],
            device_id=(to, comp), device_id_type=MESH,
        )
        for b, to in ((0, after), (1, before))
    ]
    for copy in halos:
        copy.start()

    low = jnp.full((rows, lanes), -1, jnp.int32)
    high = low
    far = lane + lanes
    for j in range(lanes):
        turned = wet_column if j == 0 else pltpu.roll(wet_column, j, 1)
        slot = (lane - j) & (lanes - 1)
        low = jnp.where(turned == lane, slot, low)
        high = jnp.where(turned == far, slot, high)
    inv[0, inner, :] = low
    inv[1, inner, :] = high

    for b in range(2):
        rows_at = slice(7 + 2 * b, 7 + 2 * b + rows)
        found = take_wide(inv[0, rows_at, :], inv[1, rows_at, :], column)
        index = jnp.maximum(found, 0)
        nbr[b] = index
        for i in range(2):
            sx[2 * i + b] = jnp.where(found >= 0, take(spd[i, rows_at, :], index), 0.0) * water
        shifted = column - 1 + 2 * b
        inside = (shifted >= 0) & (shifted < 2 * lanes)
        found = jnp.where(inside, take_wide(low, high, shifted & (2 * lanes - 1)), -1)
        index = jnp.maximum(found, 0)
        nbr[2 + b] = index
        for i in range(2):
            sy[2 * i + b] = jnp.where(found >= 0, take(spd[i, inner, :], index), 0.0) * water

    def advect_one(k, m0, m1):
        f = (first + k) // ND
        d = (first + k) % ND
        i = f - f0
        bx = (d + 8) // 16 % 2
        by = d // 16
        cos = jnp.abs(const_s[d])
        sin = jnp.abs(const_s[ND + d])
        weight = const_s[2 * ND + NF + f]
        energy = e[k, inner, :]
        gx = take(e[k, pl.ds(7 + 2 * bx, rows), :], nbr[bx])
        gy = take(energy, nbr[2 + by])
        moved = energy * (water_v[...] - (cos + sin) * spd[i, inner, :])
        moved = moved + cos * (sx[2 * i + bx] * gx) + sin * (sy[2 * i + by] * gy)
        p_ref[k] = moved
        coef[bx * 2 + i, pl.ds(k, 1), :] = jnp.full((1, lanes), cos)
        return m0 + weight * moved, m1 + (weight * const_s[2 * ND + f]) * moved

    unroll = 3

    def advect(step, carry):
        m0, m1 = carry
        for u in range(unroll):
            m0, m1 = advect_one(step * unroll + u, m0, m1)
        return m0, m1

    zero = jnp.zeros((rows, lanes), jnp.float32)
    m0, m1 = lax.fori_loop(0, comps // unroll, advect, (zero, zero))
    for n in range(GROUP):
        part[n, 0] = m0[8 * n : 8 * n + 8]
        part[n, 1] = m1[8 * n : 8 * n + 8]

    def scatter(n):
        return pltpu.make_async_remote_copy(
            src_ref=part.at[n], dst_ref=part_in.at[q], send_sem=a_send.at[n], recv_sem=a_recv.at[q],
            device_id=(tile, y * GROUP + n), device_id_type=MESH,
        )

    def send_part(n):
        @pl.when(q != n)
        def _():
            scatter(n).start()

    for n in range(1, GROUP - 1):
        send_part(n)

    for copy in halos:
        copy.wait()
    sub = lax.broadcasted_iota(jnp.int32, (8, lanes), 0)
    lane8 = lane[:8]
    their = jnp.where(
        sub == 0, halo_in[0, comps : comps + 1, :], halo_in[1, comps : comps + 1, :]
    )
    ours = jnp.where(sub == 0, col_v[0:1, :], col_v[rows - 1 : rows, :]).astype(jnp.float32)
    match = jnp.full((8, lanes), -1, jnp.int32)
    for j in range(lanes):
        turned = their if j == 0 else pltpu.roll(their, j, 1)
        match = jnp.where(turned == ours, (lane8 - j) & (lanes - 1), match)
    live = (
        ((tile + tiles - 1) // tiles).astype(jnp.float32),
        ((2 * tiles - 2 - tile) // tiles).astype(jnp.float32),
    )
    pad = halo_in.shape[1]
    for b, at in ((0, 0), (1, rows - 1)):
        found = jnp.broadcast_to(match[b : b + 1], (pad, lanes))
        scale = water_v[at : at + 1, :] * live[b]
        came = jnp.where(found >= 0, take(halo_in[b], jnp.maximum(found, 0)), 0.0) * scale
        c0 = came * coef[2 * b]
        c1 = came * coef[2 * b + 1]
        halo_out[b] = c0 + c1
        s0 = jnp.sum(c0[:comps], axis=0, keepdims=True)
        s1 = jnp.sum(c1[:comps], axis=0, keepdims=True)
        w0 = const_s[2 * ND + NF + f0]
        w1 = const_s[2 * ND + NF + f1]
        d0 = w0 * s0 + w1 * s1
        d1 = (w0 * const_s[2 * ND + f0]) * s0 + (w1 * const_s[2 * ND + f1]) * s1
        n = at // 8
        here = sub == at % 8
        part[n, 0] += jnp.where(here, d0, 0.0)
        part[n, 1] += jnp.where(here, d1, 0.0)
        send_part(n)

    copies[7].wait()
    copies[8].wait()
    wind = take_wide(wind_v[:, :lanes], wind_v[:, lanes:], column)
    angle = take_wide(angle_v[:, :lanes], angle_v[:, lanes:], column)
    wx[...] = 0.05 * wind * jnp.cos(angle)
    wy[...] = 0.05 * wind * jnp.sin(angle)

    for k in range(comps):
        bx = ((first + k) % ND + 8) // 16 % 2
        p_ref[k, pl.ds((rows - 1) * bx, 1), :] += halo_out[bx, k : k + 1, :]

    def sources(step, carry):
        for u in range(unroll):
            k = step * unroll + u
            f = (first + k) // ND
            d = (first + k) % ND
            freq = const_s[2 * ND + f]
            push = jnp.maximum((freq * const_s[d]) * wx[...] + (freq * const_s[ND + d]) * wy[...] - 0.05, 0.0)
            p_ref[k] = p_ref[k] * jnp.exp(push - fri[f - f0])
        return carry

    lax.fori_loop(0, comps // unroll, sources, 0)

    a0 = part[q, 0]
    a1 = part[q, 1]
    for o in range(1, GROUP):
        source = (q + GROUP - o) % GROUP
        pltpu.make_async_remote_copy(
            src_ref=part.at[o], dst_ref=part_in.at[source], send_sem=a_send.at[o], recv_sem=a_recv.at[source],
            device_id=(tile, y * GROUP + (q + o) % GROUP), device_id_type=MESH,
        ).wait_recv()
        a0 += part_in[source, 0]
        a1 += part_in[source, 1]
    total[0] = a0
    total[1] = a1

    exchanges = [
        pltpu.make_async_remote_copy(
            src_ref=total, dst_ref=total_in.at[y], send_sem=b_send.at[o], recv_sem=b_recv.at[y],
            device_id=(tile, (y + o) % y_count * GROUP + q), device_id_type=MESH,
        )
        for o in range(1, y_count)
    ]
    for copy in exchanges:
        copy.start()
    for o in range(1, y_count):
        source = (y + y_count - o) % y_count
        pltpu.make_async_remote_copy(
            src_ref=total, dst_ref=total_in.at[source], send_sem=b_send.at[o], recv_sem=b_recv.at[source],
            device_id=(tile, (y + o) % y_count * GROUP + q), device_id_type=MESH,
        ).wait_recv()
        a0 += total_in[source, 0]
        a1 += total_in[source, 1]

    wet_here = water_v[pl.ds(pl.multiple_of(q * 8, 8), 8), :] > 0
    mean = jnp.where(wet_here, a1 / jnp.where(wet_here, a0, 1.0), 1.0)
    square = mean * mean
    alpha = a0 * (square * square)
    mine = 2.0 * alpha * alpha / mean
    damp_out[...] = mine
    gathers = [
        pltpu.make_async_remote_copy(
            src_ref=damp_out, dst_ref=damp.at[q], send_sem=c_send.at[o], recv_sem=c_recv.at[q],
            device_id=(tile, y * GROUP + (q + o) % GROUP), device_id_type=MESH,
        )
        for o in range(1, GROUP)
    ]
    for copy in gathers:
        copy.start()
    damp[q] = mine
    for o in range(1, GROUP):
        source = (q + GROUP - o) % GROUP
        pltpu.make_async_remote_copy(
            src_ref=damp_out, dst_ref=damp.at[source], send_sem=c_send.at[o], recv_sem=c_recv.at[source],
            device_id=(tile, y * GROUP + (q + o) % GROUP), device_id_type=MESH,
        ).wait_recv()
    factor = damp[...].reshape(rows, lanes)
    x_ref[0] = jnp.exp(-const_s[2 * ND + f0] * factor)
    x_ref[1] = jnp.exp(-const_s[2 * ND + f1] * factor)

    for n in range(GROUP):
        @pl.when(q != n)
        def _():
            scatter(n).wait_send()
    for copy in exchanges:
        copy.wait_send()
    for copy in gathers:
        copy.wait_send()


def body(tiles, y_count, spectrum, sea_mask, sea_order, depth_class, wind_speed, wind_angle, speed_table, friction_table):
    comps = spectrum.shape[0]
    rows = sea_mask.shape[0]
    f32, i32 = jnp.float32, jnp.int32
    hbm = pl.BlockSpec(memory_space=pltpu.HBM)
    vmem = pl.BlockSpec(memory_space=pltpu.VMEM)
    grid = (rows, LANES)
    wide = (rows, 2 * LANES)
    pad = -(-(comps + 1) // 8) * 8
    V, S, D = pltpu.VMEM, pltpu.SMEM, pltpu.SemaphoreType.DMA
    table = jnp.asarray(constants())
    operands = (
        spectrum.reshape(comps, rows, LANES), sea_order.reshape(grid), sea_mask, depth_class, wind_speed, wind_angle,
        speed_table, friction_table, table,
    )
    p, x = pl.pallas_call(
        functools.partial(step_kernel, tiles, y_count),
        out_shape=(jax.ShapeDtypeStruct((comps,) + grid, f32), jax.ShapeDtypeStruct((2,) + grid, f32)),
        in_specs=[hbm] * 9,
        out_specs=(vmem, vmem),
        scratch_shapes=[
            S(speed_table.shape, f32), S(friction_table.shape, f32), S(table.shape, f32),
            V((comps, rows + 16, LANES), f32), V(grid, i32), V(wide, i32), V(wide, i32), V(wide, f32), V(wide, f32),
            V(grid, i32), V(grid, f32), V((2, rows + 16, LANES), i32), V((4,) + grid, i32),
            V((2, rows + 16, LANES), f32), V((4,) + grid, f32), V((4,) + grid, f32), V((2,) + grid, f32),
            V(grid, f32), V(grid, f32), V((4, pad, LANES), f32), V((2, pad, LANES), f32), V((2, pad, LANES), f32),
            V((GROUP, 2, 8, LANES), f32), V((GROUP, 2, 8, LANES), f32),
            V((2, 8, LANES), f32), V((y_count, 2, 8, LANES), f32),
            V((8, LANES), f32), V((GROUP, 8, LANES), f32),
            D((9,)), D((2,)), D((2,)), D((GROUP,)), D((GROUP,)), D((y_count,)), D((y_count,)), D((GROUP,)), D((GROUP,)),
        ],
        compiler_params=pltpu.CompilerParams(collective_id=0, has_side_effects=True, vmem_limit_bytes=32 << 20),
        name="wave_step",
    )(*[pltpu.with_memory_space_constraint(z, pltpu.HBM) for z in operands])
    first = lax.axis_index("comp") * comps
    second = (first + jnp.arange(comps)) // ND > first // ND
    result = p * jnp.where(second[:, None, None], x[1][None], x[0][None])
    return result.reshape(spectrum.shape)


def solution(mesh):
    return jax.shard_map(
        functools.partial(body, mesh.shape["tile"], mesh.shape["comp"] // GROUP),
        mesh=mesh,
        in_specs=(
            P("comp", "tile", None),
            P("tile", None),
            P("tile", None),
            P("tile", None),
            P("tile", None),
            P("tile", None),
            P(),
            P(),
        ),
        out_specs=P("comp", "tile", None),
        check_vma=False,
    )
```

time: 41.3 us -> 31.6 us (0.77)
  local copies, waits for them, and re-layouts: 5.15 us -> 0.01 us
  Pallas kernels: 34.7 us -> 30.5 us
    unnamed x18 -> x0, local copies, waits for them, and re-layouts: 5.15 us -> none
    pallas_call x1, Pallas kernels: 34.7 us -> 30.5 us  [body(): pl.pallas_call(functools.partial(step_kernel, tiles, y_count), out_shape=...]
where the time goes in v2:
time: 31.6 us; the launch traced here: 31.5 us
  Pallas kernels  30.5 us (97%)
  other arithmetic  0.95 us (3%)
    pallas_call x1, Pallas kernels, body(): pl.pallas_call(functools.partial(step_kernel, tiles, y_count), out_shape=...  30.5 us
    mul x1, other arithmetic, body(): result = p * jnp.where(second[:, None, None], x[1][None], x[0][None])  0.93 us

profile of v2, /device:TPU:1, one launch (start us, length us, event | category | flops | bytes accessed | tf_op | source)
XLA Modules:
  0.0 31.5 jit_solution(8406878165678093306)
XLA Ops:
  0.0 30.5 %wave_step.1 = (f32[18,64,128]{2,1,0:T(8,128)S(1)}, f32[2,64,128]{2,1,0:T(8,128)S(1)}) custom-call(f32[18,64,128]{2,1,0:T(8,128)} %bitcast.7, s32[64,128]{1,0:T(8,128)} %bitcast.8, s32[64,256]{1,0:T(8,128)} %mask_hbm.1, s32[64,256]{1,0:T(8,128)} %depth_hbm.1, f32[64,256]{1,0:T(8,128)} %wind_hbm.1, f32[64,256]{1,0:T(8,128)} %angle_hbm.1, f32[8,36]{1,0:T(8,128)} %speed_hbm.1, ...), custom_call_target="tpu_custom_call" | custom-call | tf_op jit(solution)/shard_map/wave_step/pallas_call | solution.py:339
  30.6 0.9 %select_multiply_fusion = f32[18,64,128]{2,1,0:T(8,128)} fusion(f32[18,64,128]{2,1,0:T(8,128)S(1)} %get-tuple-element.7, f32[64,128]{1,0:T(8,128)S(1)} %get-tuple-element.10, f32[64,128]{1,0:T(8,128)S(1)} %get-tuple-element.9, pred[18]{0:T(512)(128)(4,1)S(1)} %fusion), kind=kLoop, calls=%fused_computation | loop fusion | flops 294912 | bytes 1245202 | tf_op jit(solution)/shard_map/mul | solution.py:360
  (2 shorter events, 0.0 us)

commit v3 on v2

v3 whole, which is shorter than its diff:
```python
import functools
import math

import jax
import jax.numpy as jnp
import numpy as np
from jax import lax
from jax.experimental import pallas as pl
from jax.experimental.pallas import tpu as pltpu
from jax.sharding import PartitionSpec as P

NF = 36
ND = 32
LANES = 128
GROUP = 8
MESH = pl.DeviceIdType.MESH


def constants():
    theta = (np.arange(ND) + 0.5) * (2.0 * math.pi / ND)
    freq = 0.04 * np.exp(np.arange(NF) * (math.log(28.0) / (NF - 1)))
    weight = 0.1 * freq * (2.0 * math.pi / ND)
    return np.concatenate([np.cos(theta), np.sin(theta), freq, weight]).astype(np.float32)


def take(x, index):
    return jnp.take_along_axis(x, index, axis=1, mode="promise_in_bounds")


def take_wide(low, high, column):
    index = column & (LANES - 1)
    return jnp.where(column >= LANES, take(high, index), take(low, index))


def step_kernel(
    tiles, y_count,
    spectrum_hbm, order_hbm, mask_hbm, depth_hbm, wind_hbm, angle_hbm, speed_hbm, friction_hbm, const_hbm,
    p_ref, x_ref,
    speed_s, friction_s, const_s,
    e, order_v, mask_v, depth_v, wind_v, angle_v,
    col_v, water_v, inv, nbr, spd, sx, sy, fri, wx, wy, edge, coef, halo_out, halo_in, rim_out, rim_in,
    part, part_in, total, total_in, damp_out, damp,
    in_sem, halo_send, halo_recv, rim_send, rim_recv, a_send, a_recv, b_send, b_recv, c_send, c_recv,
):
    comps = e.shape[0]
    rows, lanes = order_v.shape
    tile = lax.axis_index("tile")
    comp = lax.axis_index("comp")
    q = lax.rem(comp, GROUP)
    y = lax.div(comp, GROUP)
    first = comp * comps
    f0 = lax.div(first, ND)
    f1 = lax.div(first + comps - 1, ND)
    has = (tile < tiles - 1, tile > 0)
    beside = (tile + 1, tile - 1)
    owner = (y * GROUP, y * GROUP + GROUP - 1)
    group = [(tile, y * GROUP + lax.rem(q + o, GROUP)) for o in range(GROUP)]
    ring = [(tile, lax.rem(y + o, y_count) * GROUP + q) for o in range(y_count)]
    order_a = sorted(range(1, GROUP), key=lambda o: abs(2 * o - GROUP))
    order_b = sorted(range(1, y_count), key=lambda o: abs(2 * o - y_count))
    inner = slice(8, rows + 8)

    copies = [
        pltpu.make_async_copy(src, dst, in_sem.at[i])
        for i, (src, dst) in enumerate(
            [(order_hbm, order_v), (mask_hbm, mask_v), (depth_hbm, depth_v),
             (speed_hbm, speed_s), (friction_hbm, friction_s), (const_hbm, const_s),
             (spectrum_hbm, e.at[:, inner, :]), (wind_hbm, wind_v), (angle_hbm, angle_v)]
        )
    ]
    for copy in copies:
        copy.start()

    barrier = pltpu.get_barrier_semaphore()
    for to in [ring[o] for o in order_b] + [group[o] for o in order_a]:
        pl.semaphore_signal(barrier, inc=1, device_id=to, device_id_type=MESH)
    for b in range(2):
        @pl.when(has[b])
        def _():
            pl.semaphore_signal(barrier, inc=1, device_id=(beside[b], comp), device_id_type=MESH)

            @pl.when(comp == owner[1 - b])
            def _():
                for n in range(GROUP):
                    pl.semaphore_signal(barrier, inc=1, device_id=(beside[b], y * GROUP + n), device_id_type=MESH)

    zero8 = jnp.zeros((8, lanes), jnp.float32)
    none8 = jnp.full((8, lanes), -1, jnp.int32)
    for pad in (slice(0, 8), slice(rows + 8, rows + 16)):
        for k in range(comps):
            e[k, pad, :] = zero8
        for h in range(2):
            inv[h, pad, :] = none8
            spd[h, pad, :] = zero8
    coef[...] = jnp.zeros_like(coef)

    for copy in copies[:5]:
        copy.wait()
    lane = lax.broadcasted_iota(jnp.int32, (rows, lanes), 1)
    row = lax.broadcasted_iota(jnp.int32, (rows, lanes), 0)
    column = order_v[...] - row * (2 * lanes)
    col_v[...] = column
    wet = take_wide(mask_v[:, :lanes], mask_v[:, lanes:], column) > 0
    water = jnp.where(wet, 1.0, 0.0)
    water_v[...] = water
    wet_column = jnp.where(wet, column, 4 * lanes)
    depth = take_wide(depth_v[:, :lanes], depth_v[:, lanes:], column)
    for i, f in enumerate((f0, f1)):
        s = jnp.full((rows, lanes), speed_s[0, f])
        r = jnp.full((rows, lanes), friction_s[0, f])
        for n in range(1, 8):
            s = jnp.where(depth == n, speed_s[n, f], s)
            r = jnp.where(depth == n, friction_s[n, f], r)
        spd[i, inner, :] = s * water
        fri[i] = r

    copies[5].wait()
    copies[6].wait()
    for k in range(comps):
        i = lax.div(first + k, ND) - f0
        d = lax.rem(first + k, ND)
        bx = lax.rem(lax.div(d + 8, 16), 2)
        coef[2 * bx + i, k : k + 1, :] = jnp.full((1, lanes), jnp.abs(const_s[d]))
        for b, at in ((0, rows - 1), (1, 0)):
            edge[b, k : k + 1, :] = e[k, 8 + at : 9 + at, :] * spd[i, 8 + at : 9 + at, :]

    low = jnp.full((rows, lanes), -1, jnp.int32)
    high = low
    far = lane + lanes
    for j in range(lanes):
        turned = wet_column if j == 0 else pltpu.roll(wet_column, j, 1)
        slot = (lane - j) & (lanes - 1)
        low = jnp.where(turned == lane, slot, low)
        high = jnp.where(turned == far, slot, high)
    inv[0, inner, :] = low
    inv[1, inner, :] = high

    for b in range(2):
        rows_at = slice(7 + 2 * b, 7 + 2 * b + rows)
        found = take_wide(inv[0, rows_at, :], inv[1, rows_at, :], column)
        index = jnp.maximum(found, 0)
        nbr[b] = index
        for i in range(2):
            sx[2 * i + b] = jnp.where(found >= 0, take(spd[i, rows_at, :], index), 0.0) * water
        shifted = column - 1 + 2 * b
        inside = (shifted >= 0) & (shifted < 2 * lanes)
        found = jnp.where(inside, take_wide(low, high, shifted & (2 * lanes - 1)), -1)
        index = jnp.maximum(found, 0)
        nbr[2 + b] = index
        for i in range(2):
            sy[2 * i + b] = jnp.where(found >= 0, take(spd[i, inner, :], index), 0.0) * water

    sub = lax.broadcasted_iota(jnp.int32, (8, lanes), 0)
    pad = edge.shape[1]
    w0 = const_s[2 * ND + NF + f0]
    w1 = const_s[2 * ND + NF + f1]
    v0 = w0 * const_s[2 * ND + f0]
    v1 = w1 * const_s[2 * ND + f1]
    for b, at in ((0, rows - 1), (1, 0)):
        near = [inv[h, 8 + at : 9 + at, :] for h in range(2)]
        for h in range(2):
            found = jnp.broadcast_to(near[h], (pad, lanes))
            halo_out[b, h] = jnp.where(found >= 0, take(edge[b], jnp.maximum(found, 0)), 0.0)
        s0 = jnp.sum((edge[b] * coef[2 * b])[:comps], axis=0, keepdims=True)
        s1 = jnp.sum((edge[b] * coef[2 * b + 1])[:comps], axis=0, keepdims=True)
        both = jnp.where(lax.rem(sub, 2) == 0, w0 * s0 + w1 * s1, v0 * s0 + v1 * s1)
        found = jnp.where(sub < 2, near[0], near[1])
        rim_out[b] = jnp.where(found >= 0, take(both, jnp.maximum(found, 0)), 0.0)

    def halo(b, to):
        return pltpu.make_async_remote_copy(
            src_ref=halo_out.at[b], dst_ref=halo_in.at[b], send_sem=halo_send.at[b], recv_sem=halo_recv.at[b],
            device_id=(to, comp), device_id_type=MESH,
        )

    def rim(b):
        return pltpu.make_async_remote_copy(
            src_ref=rim_out.at[b], dst_ref=rim_in.at[q], send_sem=rim_send.at[b], recv_sem=rim_recv.at[q],
            device_id=(beside[b], owner[b]), device_id_type=MESH,
        )

    def announce():
        sides = lax.div(tile + tiles - 1, tiles) + lax.div(2 * tiles - 2 - tile, tiles)
        pl.semaphore_wait(barrier, GROUP - 1 + y_count - 1 + 2 * sides)
        for b in range(2):
            @pl.when(has[b])
            def _():
                rim(b).start()
                halo(b, beside[b]).start()

    late = jnp.abs(2 * y - y_count) <= 2
    pl.when(late)(announce)

    def advect_one(k, m0, m1):
        f = lax.div(first + k, ND)
        d = lax.rem(first + k, ND)
        i = f - f0
        bx = lax.rem(lax.div(d + 8, 16), 2)
        by = lax.div(d, 16)
        cos = jnp.abs(const_s[d])
        sin = jnp.abs(const_s[ND + d])
        weight = const_s[2 * ND + NF + f]
        energy = e[k, inner, :]
        gx = take(e[k, pl.ds(7 + 2 * bx, rows), :], nbr[bx])
        gy = take(energy, nbr[2 + by])
        moved = energy * (water_v[...] - (cos + sin) * spd[i, inner, :])
        moved = moved + cos * (sx[2 * i + bx] * gx) + sin * (sy[2 * i + by] * gy)
        p_ref[k] = moved
        return m0 + weight * moved, m1 + (weight * const_s[2 * ND + f]) * moved

    unroll = 3

    def advect(step, carry):
        m0, m1 = carry
        for u in range(unroll):
            m0, m1 = advect_one(step * unroll + u, m0, m1)
        return m0, m1

    zero = jnp.zeros((rows, lanes), jnp.float32)
    m0, m1 = lax.fori_loop(0, comps // unroll, advect, (zero, zero))
    for n in range(GROUP):
        part[n, 0] = m0[8 * n : 8 * n + 8]
        part[n, 1] = m1[8 * n : 8 * n + 8]

    pl.when(jnp.logical_not(late))(announce)

    scatters = {
        o: pltpu.make_async_remote_copy(
            src_ref=part.at[lax.rem(q + o, GROUP)], dst_ref=part_in.at[o], send_sem=a_send.at[o], recv_sem=a_recv.at[o],
            device_id=group[o], device_id_type=MESH,
        )
        for o in order_a
    }
    for o in order_a:
        scatters[o].start()

    copies[7].wait()
    copies[8].wait()
    wind = take_wide(wind_v[:, :lanes], wind_v[:, lanes:], column)
    angle = take_wide(angle_v[:, :lanes], angle_v[:, lanes:], column)
    wx[...] = 0.05 * wind * jnp.cos(angle)
    wy[...] = 0.05 * wind * jnp.sin(angle)

    a0 = part[q, 0]
    a1 = part[q, 1]
    for o in reversed(order_a):
        scatters[o].wait_recv()
        a0 += part_in[o, 0]
        a1 += part_in[o, 1]
    total[0] = a0
    total[1] = a1
    for b, n, at in ((0, 0, 0), (1, GROUP - 1, rows - 1)):
        @pl.when(jnp.logical_and(has[1 - b], q == n))
        def _():
            came = jnp.zeros((8, lanes), jnp.float32)
            for source in range(GROUP):
                pltpu.make_async_remote_copy(
                    src_ref=rim_out.at[b], dst_ref=rim_in.at[source], send_sem=rim_send.at[b], recv_sem=rim_recv.at[source],
                    device_id=(beside[1 - b], owner[b]), device_id_type=MESH,
                ).wait_recv()
                came += rim_in[source]
            column1 = col_v[at : at + 1, :]
            found = take(came, jnp.broadcast_to(column1 & (lanes - 1), (8, lanes)))
            far_side = column1 >= lanes
            ours = water_v[at : at + 1, :]
            here = sub == at % 8
            total[0] += jnp.where(here, jnp.where(far_side, found[2:3], found[0:1]) * ours, 0.0)
            total[1] += jnp.where(here, jnp.where(far_side, found[3:4], found[1:2]) * ours, 0.0)

    exchanges = {
        o: pltpu.make_async_remote_copy(
            src_ref=total, dst_ref=total_in.at[o], send_sem=b_send.at[o], recv_sem=b_recv.at[o],
            device_id=ring[o], device_id_type=MESH,
        )
        for o in order_b
    }
    for o in order_b:
        exchanges[o].start()

    for b, at in ((0, 0), (1, rows - 1)):
        @pl.when(has[1 - b])
        def _():
            halo(b, beside[1 - b]).wait_recv()
            column1 = jnp.broadcast_to(col_v[at : at + 1, :], (pad, lanes))
            came = take_wide(halo_in[b, 0], halo_in[b, 1], column1) * water_v[at : at + 1, :]
            came = came * (coef[2 * b] + coef[2 * b + 1])
            for k in range(comps):
                p_ref[k, at : at + 1, :] += came[k : k + 1]

    def sources(step, carry):
        for u in range(unroll):
            k = step * unroll + u
            f = lax.div(first + k, ND)
            d = lax.rem(first + k, ND)
            freq = const_s[2 * ND + f]
            push = jnp.maximum((freq * const_s[d]) * wx[...] + (freq * const_s[ND + d]) * wy[...] - 0.05, 0.0)
            p_ref[k] = p_ref[k] * jnp.exp(push - fri[f - f0])
        return carry

    lax.fori_loop(0, comps // unroll, sources, 0)

    a0 = total[0]
    a1 = total[1]
    for o in reversed(order_b):
        exchanges[o].wait_recv()
        a0 += total_in[o, 0]
        a1 += total_in[o, 1]

    wet_here = water_v[pl.ds(pl.multiple_of(q * 8, 8), 8), :] > 0
    mean = jnp.where(wet_here, a1 / jnp.where(wet_here, a0, 1.0), 1.0)
    square = mean * mean
    alpha = a0 * (square * square)
    mine = 2.0 * alpha * alpha / mean
    damp_out[...] = mine
    gathers = {
        o: pltpu.make_async_remote_copy(
            src_ref=damp_out, dst_ref=damp.at[q], send_sem=c_send.at[o], recv_sem=c_recv.at[o],
            device_id=group[o], device_id_type=MESH,
        )
        for o in order_a
    }
    for o in order_a:
        gathers[o].start()
    damp[q] = mine
    for o in reversed(order_a):
        source = lax.rem(q + GROUP - o, GROUP)
        pltpu.make_async_remote_copy(
            src_ref=damp_out, dst_ref=damp.at[source], send_sem=c_send.at[o], recv_sem=c_recv.at[o],
            device_id=group[o], device_id_type=MESH,
        ).wait_recv()
    factor = damp[...].reshape(rows, lanes)
    x_ref[0] = jnp.exp(-const_s[2 * ND + f0] * factor)
    x_ref[1] = jnp.exp(-const_s[2 * ND + f1] * factor)

    for copy in [*scatters.values(), *exchanges.values(), *gathers.values()]:
        copy.wait_send()
    for b in range(2):
        @pl.when(has[b])
        def _():
            rim(b).wait_send()
            halo(b, beside[b]).wait_send()


def body(tiles, y_count, spectrum, sea_mask, sea_order, depth_class, wind_speed, wind_angle, speed_table, friction_table):
    comps = spectrum.shape[0]
    rows = sea_mask.shape[0]
    f32, i32 = jnp.float32, jnp.int32
    hbm = pl.BlockSpec(memory_space=pltpu.HBM)
    vmem = pl.BlockSpec(memory_space=pltpu.VMEM)
    grid = (rows, LANES)
    wide = (rows, 2 * LANES)
    pad = -(-comps // 8) * 8
    V, S, D = pltpu.VMEM, pltpu.SMEM, pltpu.SemaphoreType.DMA
    table = jnp.asarray(constants())
    operands = (
        spectrum.reshape(comps, rows, LANES), sea_order.reshape(grid), sea_mask, depth_class, wind_speed, wind_angle,
        speed_table, friction_table, table,
    )
    p, x = pl.pallas_call(
        functools.partial(step_kernel, tiles, y_count),
        out_shape=(jax.ShapeDtypeStruct((comps,) + grid, f32), jax.ShapeDtypeStruct((2,) + grid, f32)),
        in_specs=[hbm] * 9,
        out_specs=(vmem, vmem),
        scratch_shapes=[
            S(speed_table.shape, f32), S(friction_table.shape, f32), S(table.shape, f32),
            V((comps, rows + 16, LANES), f32), V(grid, i32), V(wide, i32), V(wide, i32), V(wide, f32), V(wide, f32),
            V(grid, i32), V(grid, f32), V((2, rows + 16, LANES), i32), V((4,) + grid, i32),
            V((2, rows + 16, LANES), f32), V((4,) + grid, f32), V((4,) + grid, f32), V((2,) + grid, f32),
            V(grid, f32), V(grid, f32), V((2, pad, LANES), f32), V((4, pad, LANES), f32),
            V((2, 2, pad, LANES), f32), V((2, 2, pad, LANES), f32), V((2, 8, LANES), f32), V((GROUP, 8, LANES), f32),
            V((GROUP, 2, 8, LANES), f32), V((GROUP, 2, 8, LANES), f32),
            V((2, 8, LANES), f32), V((y_count, 2, 8, LANES), f32),
            V((8, LANES), f32), V((GROUP, 8, LANES), f32),
            D((9,)), D((2,)), D((2,)), D((2,)), D((GROUP,)), D((GROUP,)), D((GROUP,)), D((y_count,)), D((y_count,)), D((GROUP,)), D((GROUP,)),
        ],
        compiler_params=pltpu.CompilerParams(collective_id=0, has_side_effects=True, vmem_limit_bytes=32 << 20),
        name="wave_step",
    )(*[pltpu.with_memory_space_constraint(z, pltpu.HBM) for z in operands])
    first = lax.axis_index("comp") * comps
    second = (first + jnp.arange(comps)) // ND > first // ND
    result = p * jnp.where(second[:, None, None], x[1][None], x[0][None])
    return result.reshape(spectrum.shape)


def solution(mesh):
    return jax.shard_map(
        functools.partial(body, mesh.shape["tile"], mesh.shape["comp"] // GROUP),
        mesh=mesh,
        in_specs=(
            P("comp", "tile", None),
            P("tile", None),
            P("tile", None),
            P("tile", None),
            P("tile", None),
            P("tile", None),
            P(),
            P(),
        ),
        out_specs=P("comp", "tile", None),
        check_vma=False,
    )
```

time: 31.6 us -> 24.6 us (0.78)
  Pallas kernels: 30.5 us -> 23.5 us
    pallas_call x1, Pallas kernels: 30.5 us -> 23.5 us  [body(): pl.pallas_call(functools.partial(step_kernel, tiles, y_count), out_shape=...]
where the time goes in v3:
time: 24.6 us; the launch traced here: 24.4 us
  Pallas kernels  23.5 us (96%)
  other arithmetic  0.95 us (4%)
    pallas_call x1, Pallas kernels, body(): pl.pallas_call(functools.partial(step_kernel, tiles, y_count), out_shape=...  23.5 us
    mul x1, other arithmetic, body(): result = p * jnp.where(second[:, None, None], x[1][None], x[0][None])  0.93 us

profile of v3, /device:TPU:1, one launch (start us, length us, event | category | flops | bytes accessed | tf_op | source)
XLA Modules:
  0.0 24.4 jit_solution(15849346669933029509)
XLA Ops:
  0.0 23.5 %wave_step.1 = (f32[18,64,128]{2,1,0:T(8,128)S(1)}, f32[2,64,128]{2,1,0:T(8,128)S(1)}) custom-call(f32[18,64,128]{2,1,0:T(8,128)} %bitcast.7, s32[64,128]{1,0:T(8,128)} %bitcast.8, s32[64,256]{1,0:T(8,128)} %mask_hbm.1, s32[64,256]{1,0:T(8,128)} %depth_hbm.1, f32[64,256]{1,0:T(8,128)} %wind_hbm.1, f32[64,256]{1,0:T(8,128)} %angle_hbm.1, f32[8,36]{1,0:T(8,128)} %speed_hbm.1, ...), custom_call_target="tpu_custom_call" | custom-call | tf_op jit(solution)/shard_map/wave_step/pallas_call | solution.py:359
  23.5 0.9 %select_multiply_fusion = f32[18,64,128]{2,1,0:T(8,128)} fusion(f32[18,64,128]{2,1,0:T(8,128)S(1)} %get-tuple-element.7, f32[64,128]{1,0:T(8,128)S(1)} %get-tuple-element.10, f32[64,128]{1,0:T(8,128)S(1)} %get-tuple-element.9, pred[18]{0:T(512)(128)(4,1)S(1)} %fusion), kind=kLoop, calls=%fused_computation | loop fusion | flops 294912 | bytes 1245202 | tf_op jit(solution)/shard_map/mul | solution.py:381
  (2 shorter events, 0.0 us)

commit v4 on v3

v4 whole, which is shorter than its diff:
```python
import functools
import math

import jax
import jax.numpy as jnp
import numpy as np
from jax import lax
from jax.experimental import pallas as pl
from jax.experimental.pallas import tpu as pltpu
from jax.sharding import PartitionSpec as P

NF = 36
ND = 32
LANES = 128
GROUP = 8
MESH = pl.DeviceIdType.MESH


def constants():
    theta = (np.arange(ND) + 0.5) * (2.0 * math.pi / ND)
    freq = 0.04 * np.exp(np.arange(NF) * (math.log(28.0) / (NF - 1)))
    weight = 0.1 * freq * (2.0 * math.pi / ND)
    return np.concatenate([np.cos(theta), np.sin(theta), freq, weight]).astype(np.float32)


def take(x, index):
    return lax.gather(
        x, index[..., None],
        lax.GatherDimensionNumbers((), (1,), (1,), (0,), (0,)),
        (1, 1), mode=lax.GatherScatterMode.PROMISE_IN_BOUNDS,
    )


def take_wide(low, high, column):
    index = column & (LANES - 1)
    return jnp.where(column >= LANES, take(high, index), take(low, index))


def step_kernel(
    tiles, y_count,
    spectrum_hbm, order_hbm, mask_hbm, depth_hbm, wind_hbm, angle_hbm, speed_hbm, friction_hbm, const_hbm, cos_hbm,
    p_ref, x_ref,
    speed_s, friction_s, const_s,
    cos_v, e, order_v, mask_v, depth_v, wind_v, angle_v,
    col_v, water_v, wet_v, inv, nbr, nbr_mask, spd, fri, wx, wy, edge, coef, halo_out, halo_in, rim_out, rim_in, rim_sum, rim_all,
    part, part_in, total, total_in, damp_out, damp,
    ready, in_sem, halo_send, halo_recv, rim_send, rim_recv, r_send, r_recv, a_send, a_recv, b_send, b_recv, c_send, c_recv,
):
    comps = e.shape[0]
    rows, lanes = order_v.shape
    tile = lax.axis_index("tile")
    comp = lax.axis_index("comp")
    q = lax.rem(comp, GROUP)
    y = lax.div(comp, GROUP)
    first = comp * comps
    f0 = lax.div(first, ND)
    f1 = lax.div(first + comps - 1, ND)
    has = (tile < tiles - 1, tile > 0)
    beside = (tile + 1, tile - 1)
    group = [(tile, y * GROUP + lax.rem(q + o, GROUP)) for o in range(GROUP)]
    ring = [(tile, lax.rem(y + o, y_count) * GROUP + q) for o in range(y_count)]
    order_a = sorted(range(1, GROUP), key=lambda o: abs(2 * o - GROUP))
    order_b = sorted(range(1, y_count), key=lambda o: abs(2 * o - y_count))
    inner = slice(8, rows + 8)

    copies = [
        pltpu.make_async_copy(src, dst, in_sem.at[i])
        for i, (src, dst) in enumerate(
            [(order_hbm, order_v), (mask_hbm, mask_v), (depth_hbm, depth_v),
             (wind_hbm, wind_v), (angle_hbm, angle_v), (speed_hbm, speed_s), (friction_hbm, friction_s),
             (const_hbm, const_s), (spectrum_hbm, e.at[:, inner, :]), (cos_hbm, cos_v)]
        )
    ]
    for copy in copies:
        copy.start()

    barrier = pltpu.get_barrier_semaphore()
    for to in [ring[o] for o in order_b] + [group[o] for o in order_a]:
        pl.semaphore_signal(barrier, inc=1, device_id=to, device_id_type=MESH)
    @pl.when(has[0])
    def _():
        for n in range(GROUP):
            pl.semaphore_signal(barrier, inc=1, device_id=(beside[0], y * GROUP + n), device_id_type=MESH)

    zero8 = jnp.zeros((8, lanes), jnp.float32)
    none8 = jnp.full((8, lanes), -1, jnp.int32)
    for pad in (slice(0, 8), slice(rows + 8, rows + 16)):
        for k in range(comps):
            e[k, pad, :] = zero8
        for h in range(2):
            inv[h, pad, :] = none8
            spd[h, pad, :] = zero8

    for copy in copies[:8]:
        copy.wait()
    copies[9].wait()
    sub = lax.broadcasted_iota(jnp.int32, (8, lanes), 0)
    spot = lax.broadcasted_iota(jnp.int32, (8, lanes), 1)
    groups = [slice(8 * n, 8 * n + 8) for n in range(GROUP)]
    inners = [slice(8 * n + 8, 8 * n + 16) for n in range(GROUP)]
    classes = [
        [(speed_s[n, f], friction_s[n, f]) for n in range(8)] for f in (f0, f1)
    ]
    for n, at in enumerate(groups):
        column = order_v[at, :] - (sub + 8 * n) * (2 * lanes)
        index = column & (lanes - 1)
        upper = column >= lanes
        cell = [
            jnp.where(upper, take(v[at, lanes:], index), take(v[at, :lanes], index))
            for v in (mask_v, depth_v, wind_v, angle_v)
        ]
        wet = cell[0] > 0
        water = jnp.where(wet, 1.0, 0.0)
        col_v[at, :] = column
        water_v[at, :] = water
        wet_v[at, :] = jnp.where(wet, column, 4 * lanes)
        wx[at, :] = cell[2]
        wy[at, :] = cell[3]
        s = [jnp.full((8, lanes), c[0][0]) for c in classes]
        r = [jnp.full((8, lanes), c[0][1]) for c in classes]
        for m in range(1, 8):
            here = cell[1] == m
            for i in range(2):
                s[i] = jnp.where(here, classes[i][m][0], s[i])
                r[i] = jnp.where(here, classes[i][m][1], r[i])
        for i in range(2):
            spd[i, inners[n], :] = s[i] * water
            fri[i, at, :] = r[i]

    narrow = jnp.int16
    lane = lax.broadcasted_iota(jnp.int32, (rows, lanes), 1)
    near = lane.astype(narrow)
    far = (lane + lanes).astype(narrow)
    here = wet_v[...].astype(narrow)
    low = jnp.full((rows, lanes), -1, narrow)
    high = low
    for j in range(lanes):
        turned = here if j == 0 else pltpu.roll(here, j, 1)
        slot = ((lane - j) & (lanes - 1)).astype(narrow)
        low = jnp.where(turned == near, slot, low)
        high = jnp.where(turned == far, slot, high)
    inv[0, inner, :] = low.astype(jnp.int32)
    inv[1, inner, :] = high.astype(jnp.int32)

    for n, at in enumerate(groups):
        column = col_v[at, :]
        water = water_v[at, :]
        index = column & (lanes - 1)
        upper = column >= lanes
        for b in range(2):
            rows_at = slice(8 * n + 7 + 2 * b, 8 * n + 15 + 2 * b)
            found = jnp.where(upper, take(inv[1, rows_at, :], index), take(inv[0, rows_at, :], index))
            nbr[b, at, :] = jnp.maximum(found, 0)
            nbr_mask[b, at, :] = jnp.where(found >= 0, water, 0.0)
        for b in range(2):
            shifted = column - 1 + 2 * b
            index = shifted & (lanes - 1)
            found = jnp.where(shifted >= lanes, take(inv[1, inners[n], :], index), take(inv[0, inners[n], :], index))
            inside = (shifted >= 0) & (shifted < 2 * lanes) & (found >= 0)
            nbr[2 + b, at, :] = jnp.maximum(found, 0)
            nbr_mask[2 + b, at, :] = jnp.where(inside, water, 0.0)

    copies[8].wait()
    pad = edge.shape[1]
    comp_at = first + lax.broadcasted_iota(jnp.int32, (pad, lanes), 0)
    second = comp_at >= ND * (f0 + 1)
    turn = (((comp_at & (ND - 1)) + 8) >> 4) & 1
    spread = jnp.abs(cos_v[pl.ds(lax.rem(first, ND), pad), :])
    for b in range(2):
        for i in range(2):
            coef[2 * b + i] = jnp.where((turn == b) & (second == (i == 1)), spread, 0.0)
    for b, at in ((0, rows - 1), (1, 0)):
        speed = jnp.where(second, spd[1, 8 + at : 9 + at, :], spd[0, 8 + at : 9 + at, :])
        edge[b, :comps, :] = e[:, 8 + at, :] * speed[:comps]

    w0 = const_s[2 * ND + NF + f0]
    w1 = const_s[2 * ND + NF + f1]
    v0 = w0 * const_s[2 * ND + f0]
    v1 = w1 * const_s[2 * ND + f1]
    for b, at in ((0, rows - 1), (1, 0)):
        back = [inv[h, 8 + at : 9 + at, :] for h in range(2)]
        for h in range(2):
            found = jnp.broadcast_to(back[h], (pad, lanes))
            halo_out[b, h] = jnp.where(found >= 0, take(edge[b], jnp.maximum(found, 0)), 0.0)
        s0 = jnp.sum((edge[b] * coef[2 * b])[:comps], axis=0, keepdims=True)
        s1 = jnp.sum((edge[b] * coef[2 * b + 1])[:comps], axis=0, keepdims=True)
        both = jnp.where(lax.rem(sub, 2) == 0, w0 * s0 + w1 * s1, v0 * s0 + v1 * s1)
        found = jnp.where(sub < 2, back[0], back[1])
        rim_out[b] = jnp.where(found >= 0, take(both, jnp.maximum(found, 0)), 0.0)

    def halo(b, to):
        return pltpu.make_async_remote_copy(
            src_ref=halo_out.at[b], dst_ref=halo_in.at[b], send_sem=halo_send.at[b], recv_sem=halo_recv.at[b],
            device_id=(to, comp), device_id_type=MESH,
        )

    def rim(b, n):
        return pltpu.make_async_remote_copy(
            src_ref=rim_out.at[b], dst_ref=rim_in.at[b, q], send_sem=rim_send.at[b], recv_sem=rim_recv.at[b],
            device_id=(beside[b], y * GROUP + n), device_id_type=MESH,
        )

    def drain(ref, sem):
        pltpu.make_async_copy(ref, ref, sem).wait()

    def send_beside(b):
        for n in (3, 4, 2, 5, 1, 6, 0, 7):
            rim(b, n).start()
        halo(b, beside[b]).start()

    def announce():
        pl.semaphore_wait(barrier, GROUP - 1 + y_count - 1 + GROUP * lax.div(tile + tiles - 1, tiles))

        @pl.when(has[1])
        def _():
            for n in range(GROUP):
                pl.semaphore_signal(ready, inc=1, device_id=(beside[1], y * GROUP + n), device_id_type=MESH)
            send_beside(1)

    late = jnp.abs(2 * y - y_count) <= 2
    pl.when(late)(announce)

    def advect(step, carry):
        sums = list(carry)
        for pair in range(3):
            advect_pair(6 * step + 2 * pair, sums)
        return tuple(sums)

    def advect_pair(k, sums):
        f = lax.div(first + k, ND)
        d = lax.rem(first + k, ND)
        i = f - f0
        bx = lax.rem(lax.div(d + 8, 16), 2)
        by = lax.div(d, 16)
        weight = const_s[2 * ND + NF + f]
        weight_freq = weight * const_s[2 * ND + f]
        cos = [jnp.abs(const_s[d + u]) for u in range(2)]
        sin = [jnp.abs(const_s[ND + d + u]) for u in range(2)]
        for n, at in enumerate(groups):
            speed = spd[i, inners[n], :]
            behind = pl.ds(8 * n + 7 + 2 * bx, 8)
            speed_x = spd[i, behind, :]
            energy = [e[k + u, inners[n], :] for u in range(2)]
            flux = [energy[u] * speed for u in range(2)]
            flux_x = [e[k + u, behind, :] * speed_x for u in range(2)]
            index = nbr[bx, at, :]
            gx = [take(flux_x[u], index) for u in range(2)]
            index = nbr[2 + by, at, :]
            gy = [take(flux[u], index) for u in range(2)]
            mask_x = nbr_mask[bx, at, :]
            mask_y = nbr_mask[2 + by, at, :]
            water = water_v[at, :]
            for u in range(2):
                moved = energy[u] * water - (cos[u] + sin[u]) * flux[u]
                moved = moved + cos[u] * (mask_x * gx[u]) + sin[u] * (mask_y * gy[u])
                p_ref[k + u, at, :] = moved
                sums[n] = sums[n] + weight * moved
                sums[GROUP + n] = sums[GROUP + n] + weight_freq * moved

    zero = jnp.zeros((8, lanes), jnp.float32)
    sums = lax.fori_loop(0, comps // 6, advect, (zero,) * (2 * GROUP))
    for n in range(GROUP):
        part[n, 0] = sums[n]
        part[n, 1] = sums[GROUP + n]

    pl.when(jnp.logical_not(late))(announce)

    scatters = {
        o: pltpu.make_async_remote_copy(
            src_ref=part.at[lax.rem(q + o, GROUP)], dst_ref=part_in.at[o - 1], send_sem=a_send, recv_sem=a_recv,
            device_id=group[o], device_id_type=MESH,
        )
        for o in order_a
    }
    for o in order_a:
        scatters[o].start()

    wind = 0.05 * wx[...]
    angle = wy[...]
    wx[...] = wind * jnp.cos(angle)
    wy[...] = wind * jnp.sin(angle)

    drain(part_in, a_recv)
    for h in range(2):
        held = part[q, h]
        for n in range(GROUP - 1):
            held += part_in[n, h]
        total[h] = held

    exchanges = {
        o: pltpu.make_async_remote_copy(
            src_ref=total, dst_ref=total_in.at[o - 1], send_sem=b_send, recv_sem=b_recv,
            device_id=ring[o], device_id_type=MESH,
        )
        for o in order_b
    }
    for o in order_b:
        exchanges[o].start()

    @pl.when(has[0])
    def _():
        pl.semaphore_wait(ready, GROUP)
        send_beside(0)

    for b, at in ((0, 0), (1, rows - 1)):
        @pl.when(has[1 - b])
        def _():
            halo(b, beside[1 - b]).wait_recv()
            column1 = jnp.broadcast_to(col_v[at : at + 1, :], (pad, lanes))
            came = take_wide(halo_in[b, 0], halo_in[b, 1], column1) * water_v[at : at + 1, :]
            came = came * (coef[2 * b] + coef[2 * b + 1])
            for k in range(comps):
                p_ref[k, at : at + 1, :] += came[k : k + 1]

    def sources(step, carry):
        for u in range(3):
            k = step * 3 + u
            f = lax.div(first + k, ND)
            d = lax.rem(first + k, ND)
            freq = const_s[2 * ND + f]
            push = jnp.maximum((freq * const_s[d]) * wx[...] + (freq * const_s[ND + d]) * wy[...] - 0.05, 0.0)
            p_ref[k] = p_ref[k] * jnp.exp(push - fri[f - f0])
        return carry

    lax.fori_loop(0, comps // 3, sources, 0)

    for b in range(2):
        rim_sum[b] = jnp.zeros((8, lanes), jnp.float32)

        @pl.when(has[1 - b])
        def _():
            drain(rim_in.at[b], rim_recv.at[b])
            came = rim_in[b, 0]
            for n in range(1, GROUP):
                came += rim_in[b, n]
            rim_sum[b] = came

    rims = {
        o: pltpu.make_async_remote_copy(
            src_ref=rim_sum, dst_ref=rim_all.at[o - 1], send_sem=r_send, recv_sem=r_recv,
            device_id=ring[o], device_id_type=MESH,
        )
        for o in order_b
    }
    for o in order_b:
        rims[o].start()

    drain(total_in, b_recv)
    a0 = total[0]
    a1 = total[1]
    for n in range(y_count - 1):
        a0 += total_in[n, 0]
        a1 += total_in[n, 1]

    def damping(m0, m1, wet):
        mean = jnp.where(wet, m1 / jnp.where(wet, m0, 1.0), 1.0)
        square = mean * mean
        alpha = m0 * (square * square)
        return 2.0 * alpha * alpha / mean

    outer = lax.div(q, GROUP - 1)
    rim0 = jnp.where(outer == 1, a0[7:8], a0[0:1])
    rim1 = jnp.where(outer == 1, a1[7:8], a1[0:1])
    wet_here = water_v[pl.ds(pl.multiple_of(q * 8, 8), 8), :] > 0
    mine = damping(a0, a1, wet_here)
    damp_out[0] = mine
    damp_out[1] = jnp.where(sub == 0, rim0, rim1)
    gathers = {
        o: pltpu.make_async_remote_copy(
            src_ref=damp_out, dst_ref=damp.at[q], send_sem=c_send, recv_sem=c_recv,
            device_id=group[o], device_id_type=MESH,
        )
        for o in order_a
    }
    for o in order_a:
        gathers[o].start()
    damp[q, 0] = mine
    damp[q, 1] = damp_out[1]
    drain(rim_all, r_recv)
    added = []
    for b, at in ((0, 0), (1, rows - 1)):
        came = rim_sum[b]
        for n in range(y_count - 1):
            came += rim_all[n, b]
        column1 = col_v[at : at + 1, :]
        found = take(came, jnp.broadcast_to(column1 & (lanes - 1), (8, lanes)))
        ours = water_v[at : at + 1, :]
        added.append(jnp.where(column1 >= lanes, found[2:4], found[0:2]) * ours)
    drain(damp.at[pl.ds(0, GROUP - 1)], c_recv)
    factor = [damp[n, 0] for n in range(GROUP)]
    for b, n, at in ((0, 0, 0), (1, GROUP - 1, rows - 1)):
        both = damp[n, 1][0:2] + added[b]
        fixed = damping(both[0:1], both[1:2], water_v[at : at + 1, :] > 0)
        factor[n] = jnp.where(sub == at % 8, fixed, factor[n])
    for n, at in enumerate(groups):
        x_ref[0, at, :] = jnp.exp(-const_s[2 * ND + f0] * factor[n])
        x_ref[1, at, :] = jnp.exp(-const_s[2 * ND + f1] * factor[n])

    drain(part_in, a_send)
    drain(total_in, b_send)
    drain(rim_all, r_send)
    drain(damp.at[pl.ds(0, GROUP - 1)], c_send)
    for b in range(2):
        @pl.when(has[b])
        def _():
            drain(rim_in.at[b], rim_send.at[b])
            halo(b, beside[b]).wait_send()


def body(tiles, y_count, spectrum, sea_mask, sea_order, depth_class, wind_speed, wind_angle, speed_table, friction_table):
    comps = spectrum.shape[0]
    rows = sea_mask.shape[0]
    f32, i32 = jnp.float32, jnp.int32
    hbm = pl.BlockSpec(memory_space=pltpu.HBM)
    vmem = pl.BlockSpec(memory_space=pltpu.VMEM)
    grid = (rows, LANES)
    wide = (rows, 2 * LANES)
    pad = -(-comps // 8) * 8
    V, S, D = pltpu.VMEM, pltpu.SMEM, pltpu.SemaphoreType.DMA
    numbers = constants()
    table = jnp.asarray(numbers)
    doubled = jnp.asarray(np.ascontiguousarray(np.broadcast_to(np.tile(numbers[:ND], 2)[:, None], (2 * ND, LANES))))
    operands = (
        spectrum.reshape(comps, rows, LANES), sea_order.reshape(grid), sea_mask, depth_class, wind_speed, wind_angle,
        speed_table, friction_table, table, doubled,
    )
    p, x = pl.pallas_call(
        functools.partial(step_kernel, tiles, y_count),
        out_shape=(jax.ShapeDtypeStruct((comps,) + grid, f32), jax.ShapeDtypeStruct((2,) + grid, f32)),
        in_specs=[hbm] * 10,
        out_specs=(vmem, vmem),
        scratch_shapes=[
            S(speed_table.shape, f32), S(friction_table.shape, f32), S(table.shape, f32),
            V(doubled.shape, f32), V((comps, rows + 16, LANES), f32),
            V(grid, i32), V(wide, i32), V(wide, i32), V(wide, f32), V(wide, f32),
            V(grid, i32), V(grid, f32), V(grid, i32), V((2, rows + 16, LANES), i32), V((4,) + grid, i32), V((4,) + grid, f32),
            V((2, rows + 16, LANES), f32), V((2,) + grid, f32),
            V(grid, f32), V(grid, f32), V((2, pad, LANES), f32), V((4, pad, LANES), f32),
            V((2, 2, pad, LANES), f32), V((2, 2, pad, LANES), f32), V((2, 8, LANES), f32), V((2, GROUP, 8, LANES), f32),
            V((2, 8, LANES), f32), V((y_count - 1, 2, 8, LANES), f32),
            V((GROUP, 2, 8, LANES), f32), V((GROUP - 1, 2, 8, LANES), f32),
            V((2, 8, LANES), f32), V((y_count - 1, 2, 8, LANES), f32),
            V((2, 8, LANES), f32), V((GROUP, 2, 8, LANES), f32),
            pltpu.SemaphoreType.REGULAR, D((10,)), D((2,)), D((2,)), D((2,)), D((2,)), D, D, D, D, D, D, D, D,
        ],
        compiler_params=pltpu.CompilerParams(collective_id=0, has_side_effects=True, vmem_limit_bytes=32 << 20),
        name="wave_step",
    )(*[pltpu.with_memory_space_constraint(z, pltpu.HBM) for z in operands])
    first = lax.axis_index("comp") * comps
    second = (first + jnp.arange(comps)) // ND > first // ND
    result = p * jnp.where(second[:, None, None], x[1][None], x[0][None])
    return result.reshape(spectrum.shape)


def solution(mesh):
    return jax.shard_map(
        functools.partial(body, mesh.shape["tile"], mesh.shape["comp"] // GROUP),
        mesh=mesh,
        in_specs=(
            P("comp", "tile", None),
            P("tile", None),
            P("tile", None),
            P("tile", None),
            P("tile", None),
            P("tile", None),
            P(),
            P(),
        ),
        out_specs=P("comp", "tile", None),
        check_vma=False,
    )
```

time: 24.6 us -> 24.3 us (0.988)
  Pallas kernels: 23.5 us -> 23.2 us
    pallas_call x1, Pallas kernels: 23.5 us -> 23.2 us  [body(): pl.pallas_call(functools.partial(step_kernel, tiles, y_count), out_shape=...]
where the time goes in v4:
time: 24.3 us; the launch traced here: 24.2 us
  Pallas kernels  23.2 us (95%)
  other arithmetic  0.95 us (4%)
    pallas_call x1, Pallas kernels, body(): pl.pallas_call(functools.partial(step_kernel, tiles, y_count), out_shape=...  23.2 us
    mul x1, other arithmetic, body(): result = p * jnp.where(second[:, None, None], x[1][None], x[0][None])  0.93 us

profile of v4, /device:TPU:1, one launch (start us, length us, event | category | flops | bytes accessed | tf_op | source)
XLA Modules:
  0.0 24.2 jit_solution(13632123573923175764)
XLA Ops:
  0.0 23.2 %wave_step.1 = (f32[18,64,128]{2,1,0:T(8,128)S(1)}, f32[2,64,128]{2,1,0:T(8,128)S(1)}) custom-call(f32[18,64,128]{2,1,0:T(8,128)} %bitcast.7, s32[64,128]{1,0:T(8,128)} %bitcast.8, s32[64,256]{1,0:T(8,128)} %mask_hbm.1, s32[64,256]{1,0:T(8,128)} %depth_hbm.1, f32[64,256]{1,0:T(8,128)} %wind_hbm.1, f32[64,256]{1,0:T(8,128)} %angle_hbm.1, f32[8,36]{1,0:T(8,128)} %speed_hbm.1, ...), custom_call_target="tpu_custom_call" | custom-call | tf_op jit(solution)/shard_map/wave_step/pallas_call | solution.py:427
  23.3 0.9 %select_multiply_fusion = f32[18,64,128]{2,1,0:T(8,128)} fusion(f32[18,64,128]{2,1,0:T(8,128)S(1)} %get-tuple-element.7, f32[64,128]{1,0:T(8,128)S(1)} %get-tuple-element.10, f32[64,128]{1,0:T(8,128)S(1)} %get-tuple-element.9, pred[18]{0:T(512)(128)(4,1)S(1)} %fusion), kind=kLoop, calls=%fused_computation | loop fusion | flops 294912 | bytes 1245202 | tf_op jit(solution)/shard_map/mul | solution.py:451
  (2 shorter events, 0.0 us)

commit v5 on v4

--- a/solution.py
+++ b/solution.py
@@ -39,12 +39,12 @@
 def step_kernel(
     tiles, y_count,
     spectrum_hbm, order_hbm, mask_hbm, depth_hbm, wind_hbm, angle_hbm, speed_hbm, friction_hbm, const_hbm, cos_hbm,
-    p_ref, x_ref,
+    x_ref, p_ref,
     speed_s, friction_s, const_s,
     cos_v, e, order_v, mask_v, depth_v, wind_v, angle_v,
     col_v, water_v, wet_v, inv, nbr, nbr_mask, spd, fri, wx, wy, edge, coef, halo_out, halo_in, rim_out, rim_in, rim_sum, rim_all,
     part, part_in, total, total_in, damp_out, damp,
-    ready, in_sem, halo_send, halo_recv, rim_send, rim_recv, r_send, r_recv, a_send, a_recv, b_send, b_recv, c_send, c_recv,
+    ready, passed, in_sem, halo_send, halo_recv, rim_send, rim_recv, r_send, r_recv, a_send, a_recv, b_send, b_recv, c_send, c_recv,
 ):
     comps = e.shape[0]
     rows, lanes = order_v.shape
@@ -75,7 +75,7 @@
         copy.start()
 
     barrier = pltpu.get_barrier_semaphore()
-    for to in [ring[o] for o in order_b] + [group[o] for o in order_a]:
+    for to in [group[o] for o in order_a] + [ring[1], ring[y_count - 1]]:
         pl.semaphore_signal(barrier, inc=1, device_id=to, device_id_type=MESH)
     @pl.when(has[0])
     def _():
@@ -208,8 +208,14 @@
             rim(b, n).start()
         halo(b, beside[b]).start()
 
+    def relay(step):
+        for o in (step + 1, y_count - step - 1):
+            pl.semaphore_signal(passed.at[step], inc=1, device_id=ring[o], device_id_type=MESH)
+
     def announce():
-        pl.semaphore_wait(barrier, GROUP - 1 + y_count - 1 + GROUP * lax.div(tile + tiles - 1, tiles))
+        pl.semaphore_wait(barrier, GROUP + 1 + GROUP * lax.div(tile + tiles - 1, tiles))
+
+        relay(0)
 
         @pl.when(has[1])
         def _():
@@ -275,6 +281,10 @@
     for o in order_a:
         scatters[o].start()
 
+    pl.semaphore_wait(passed.at[0], 2)
+    if y_count > 4:
+        relay(1)
+
     wind = 0.05 * wx[...]
     angle = wy[...]
     wx[...] = wind * jnp.cos(angle)
@@ -287,6 +297,8 @@
             held += part_in[n, h]
         total[h] = held
 
+    if y_count > 4:
+        pl.semaphore_wait(passed.at[1], 2)
     exchanges = {
         o: pltpu.make_async_remote_copy(
             src_ref=total, dst_ref=total_in.at[o - 1], send_sem=b_send, recv_sem=b_recv,
@@ -393,8 +405,12 @@
         fixed = damping(both[0:1], both[1:2], water_v[at : at + 1, :] > 0)
         factor[n] = jnp.where(sub == at % 8, fixed, factor[n])
     for n, at in enumerate(groups):
-        x_ref[0, at, :] = jnp.exp(-const_s[2 * ND + f0] * factor[n])
-        x_ref[1, at, :] = jnp.exp(-const_s[2 * ND + f1] * factor[n])
+        wx[at, :] = jnp.exp(-const_s[2 * ND + f0] * factor[n])
+        wy[at, :] = jnp.exp(-const_s[2 * ND + f1] * factor[n])
+    for k in range(0, comps, 2):
+        fade = jnp.where(lax.div(first + k, ND) == f0, wx[...], wy[...])
+        for u in range(2):
+            x_ref[k + u] = p_ref[k + u] * fade
 
     drain(part_in, a_send)
     drain(total_in, b_send)
@@ -424,12 +440,13 @@
         spectrum.reshape(comps, rows, LANES), sea_order.reshape(grid), sea_mask, depth_class, wind_speed, wind_angle,
         speed_table, friction_table, table, doubled,
     )
-    p, x = pl.pallas_call(
+    result = pl.pallas_call(
         functools.partial(step_kernel, tiles, y_count),
-        out_shape=(jax.ShapeDtypeStruct((comps,) + grid, f32), jax.ShapeDtypeStruct((2,) + grid, f32)),
+        out_shape=jax.ShapeDtypeStruct((comps,) + grid, f32),
         in_specs=[hbm] * 10,
-        out_specs=(vmem, vmem),
+        out_specs=vmem,
         scratch_shapes=[
+            V((comps,) + grid, f32),
             S(speed_table.shape, f32), S(friction_table.shape, f32), S(table.shape, f32),
             V(doubled.shape, f32), V((comps, rows + 16, LANES), f32),
             V(grid, i32), V(wide, i32), V(wide, i32), V(wide, f32), V(wide, f32),
@@ -441,14 +458,11 @@
             V((GROUP, 2, 8, LANES), f32), V((GROUP - 1, 2, 8, LANES), f32),
             V((2, 8, LANES), f32), V((y_count - 1, 2, 8, LANES), f32),
             V((2, 8, LANES), f32), V((GROUP, 2, 8, LANES), f32),
-            pltpu.SemaphoreType.REGULAR, D((10,)), D((2,)), D((2,)), D((2,)), D((2,)), D, D, D, D, D, D, D, D,
+            pltpu.SemaphoreType.REGULAR, pltpu.SemaphoreType.REGULAR((2,)), D((10,)), D((2,)), D((2,)), D((2,)), D((2,)), D, D, D, D, D, D, D, D,
         ],
         compiler_params=pltpu.CompilerParams(collective_id=0, has_side_effects=True, vmem_limit_bytes=32 << 20),
         name="wave_step",
     )(*[pltpu.with_memory_space_constraint(z, pltpu.HBM) for z in operands])
-    first = lax.axis_index("comp") * comps
-    second = (first + jnp.arange(comps)) // ND > first // ND
-    result = p * jnp.where(second[:, None, None], x[1][None], x[0][None])
     return result.reshape(spectrum.shape)
 
 

time: 24.3 us -> 21.5 us (0.88)
  Pallas kernels: 23.2 us -> 20.5 us
  other arithmetic: 0.95 us -> 0 us
  local copies, waits for them, and re-layouts: 0.01 us -> 0.82 us
    pallas_call x1, Pallas kernels: 23.2 us -> 20.5 us  [body(): pl.pallas_call(functools.partial(step_kernel, tiles, y_count), out_shape=...]
    mul x1 -> x0, other arithmetic: 0.93 us -> none  [body(): result = p * jnp.where(second[:, None, None], x[1][None], x[0][None])]
    unnamed x0 -> x1, local copies, waits for them, and re-layouts: none -> 0.82 us
where the time goes in v5:
time: 21.5 us; the launch traced here: 21.4 us
  Pallas kernels  20.5 us (95%)
  local copies, waits for them, and re-layouts  0.82 us (4%)
    pallas_call x1, Pallas kernels, body(): pl.pallas_call(functools.partial(step_kernel, tiles, y_count), out_shape=...  20.5 us
    unnamed x1, local copies, waits for them, and re-layouts  0.82 us

profile of v5, /device:TPU:1, one launch (start us, length us, event | category | flops | bytes accessed | tf_op | source)
XLA Modules:
  0.0 21.4 jit_solution(11261327994738408071)
XLA Ops:
  0.0 20.5 %wave_step.1 = f32[18,64,128]{2,1,0:T(8,128)S(1)} custom-call(f32[18,64,128]{2,1,0:T(8,128)} %bitcast.4, s32[64,128]{1,0:T(8,128)} %bitcast.5, s32[64,256]{1,0:T(8,128)} %mask_hbm.1, s32[64,256]{1,0:T(8,128)} %depth_hbm.1, f32[64,256]{1,0:T(8,128)} %wind_hbm.1, f32[64,256]{1,0:T(8,128)} %angle_hbm.1, f32[8,36]{1,0:T(8,128)} %speed_hbm.1, ...), custom_call_target="tpu_custom_call" | custom-call | tf_op jit(solution)/shard_map/wave_step/pallas_call | solution.py:443
  20.6 0.8 %copy.14 = f32[18,1,8192]{2,1,0:T(1,128)} copy(f32[18,1,8192]{2,1,0:T(1,128)S(1)} %bitcast.3) | data formatting | bytes 1179648

commit v6 on v5

--- a/solution.py
+++ b/solution.py
@@ -83,17 +83,15 @@
             pl.semaphore_signal(barrier, inc=1, device_id=(beside[0], y * GROUP + n), device_id_type=MESH)
 
     zero8 = jnp.zeros((8, lanes), jnp.float32)
-    none8 = jnp.full((8, lanes), -1, jnp.int32)
-    for pad in (slice(0, 8), slice(rows + 8, rows + 16)):
+    for rim_rows in (slice(0, 8), slice(rows + 8, rows + 16)):
+        inv[rim_rows, :] = jnp.zeros((8, lanes), jnp.int32)
         for k in range(comps):
-            e[k, pad, :] = zero8
+            e[k, rim_rows, :] = zero8
         for h in range(2):
-            inv[h, pad, :] = none8
-            spd[h, pad, :] = zero8
-
-    for copy in copies[:8]:
+            spd[h, rim_rows, :] = zero8
+
+    for copy in copies[:3] + copies[5:8]:
         copy.wait()
-    copies[9].wait()
     sub = lax.broadcasted_iota(jnp.int32, (8, lanes), 0)
     spot = lax.broadcasted_iota(jnp.int32, (8, lanes), 1)
     groups = [slice(8 * n, 8 * n + 8) for n in range(GROUP)]
@@ -105,21 +103,18 @@
         column = order_v[at, :] - (sub + 8 * n) * (2 * lanes)
         index = column & (lanes - 1)
         upper = column >= lanes
-        cell = [
-            jnp.where(upper, take(v[at, lanes:], index), take(v[at, :lanes], index))
-            for v in (mask_v, depth_v, wind_v, angle_v)
-        ]
-        wet = cell[0] > 0
+        halves = [mask_v[at, h] + 2 * depth_v[at, h] for h in (slice(0, lanes), slice(lanes, 2 * lanes))]
+        cell = jnp.where(upper, take(halves[1], index), take(halves[0], index))
+        wet = (cell & 1) > 0
+        kind = cell >> 1
         water = jnp.where(wet, 1.0, 0.0)
         col_v[at, :] = column
         water_v[at, :] = water
         wet_v[at, :] = jnp.where(wet, column, 4 * lanes)
-        wx[at, :] = cell[2]
-        wy[at, :] = cell[3]
         s = [jnp.full((8, lanes), c[0][0]) for c in classes]
         r = [jnp.full((8, lanes), c[0][1]) for c in classes]
         for m in range(1, 8):
-            here = cell[1] == m
+            here = kind == m
             for i in range(2):
                 s[i] = jnp.where(here, classes[i][m][0], s[i])
                 r[i] = jnp.where(here, classes[i][m][1], r[i])
@@ -139,28 +134,29 @@
         slot = ((lane - j) & (lanes - 1)).astype(narrow)
         low = jnp.where(turned == near, slot, low)
         high = jnp.where(turned == far, slot, high)
-    inv[0, inner, :] = low.astype(jnp.int32)
-    inv[1, inner, :] = high.astype(jnp.int32)
+    inv[inner, :] = (low.astype(jnp.int32) + 1) | ((high.astype(jnp.int32) + 1) << 8)
 
     for n, at in enumerate(groups):
         column = col_v[at, :]
         water = water_v[at, :]
         index = column & (lanes - 1)
         upper = column >= lanes
+        got = take(inv[8 * n + 7 : 8 * n + 15, :] | (inv[8 * n + 9 : 8 * n + 17, :] << 16), index)
+        got = jnp.where(upper, got >> 8, got)
         for b in range(2):
-            rows_at = slice(8 * n + 7 + 2 * b, 8 * n + 15 + 2 * b)
-            found = jnp.where(upper, take(inv[1, rows_at, :], index), take(inv[0, rows_at, :], index))
+            found = ((got >> 16 if b else got) & 255) - 1
             nbr[b, at, :] = jnp.maximum(found, 0)
             nbr_mask[b, at, :] = jnp.where(found >= 0, water, 0.0)
         for b in range(2):
             shifted = column - 1 + 2 * b
-            index = shifted & (lanes - 1)
-            found = jnp.where(shifted >= lanes, take(inv[1, inners[n], :], index), take(inv[0, inners[n], :], index))
+            got = take(inv[inners[n], :], shifted & (lanes - 1))
+            found = (jnp.where(shifted >= lanes, got >> 8, got) & 255) - 1
             inside = (shifted >= 0) & (shifted < 2 * lanes) & (found >= 0)
             nbr[2 + b, at, :] = jnp.maximum(found, 0)
             nbr_mask[2 + b, at, :] = jnp.where(inside, water, 0.0)
 
     copies[8].wait()
+    copies[9].wait()
     pad = edge.shape[1]
     comp_at = first + lax.broadcasted_iota(jnp.int32, (pad, lanes), 0)
     second = comp_at >= ND * (f0 + 1)
@@ -178,7 +174,8 @@
     v0 = w0 * const_s[2 * ND + f0]
     v1 = w1 * const_s[2 * ND + f1]
     for b, at in ((0, rows - 1), (1, 0)):
-        back = [inv[h, 8 + at : 9 + at, :] for h in range(2)]
+        packed = inv[8 + at : 9 + at, :]
+        back = [(packed & 255) - 1, (packed >> 8) - 1]
         for h in range(2):
             found = jnp.broadcast_to(back[h], (pad, lanes))
             halo_out[b, h] = jnp.where(found >= 0, take(edge[b], jnp.maximum(found, 0)), 0.0)
@@ -285,10 +282,16 @@
     if y_count > 4:
         relay(1)
 
-    wind = 0.05 * wx[...]
-    angle = wy[...]
-    wx[...] = wind * jnp.cos(angle)
-    wy[...] = wind * jnp.sin(angle)
+    copies[3].wait()
+    copies[4].wait()
+    for at in groups:
+        column = col_v[at, :]
+        index = column & (lanes - 1)
+        upper = column >= lanes
+        wind = 0.05 * jnp.where(upper, take(wind_v[at, lanes:], index), take(wind_v[at, :lanes], index))
+        angle = jnp.where(upper, take(angle_v[at, lanes:], index), take(angle_v[at, :lanes], index))
+        wx[at, :] = wind * jnp.cos(angle)
+        wy[at, :] = wind * jnp.sin(angle)
 
     drain(part_in, a_recv)
     for h in range(2):
@@ -450,7 +453,7 @@
             S(speed_table.shape, f32), S(friction_table.shape, f32), S(table.shape, f32),
             V(doubled.shape, f32), V((comps, rows + 16, LANES), f32),
             V(grid, i32), V(wide, i32), V(wide, i32), V(wide, f32), V(wide, f32),
-            V(grid, i32), V(grid, f32), V(grid, i32), V((2, rows + 16, LANES), i32), V((4,) + grid, i32), V((4,) + grid, f32),
+            V(grid, i32), V(grid, f32), V(grid, i32), V((rows + 16, LANES), i32), V((4,) + grid, i32), V((4,) + grid, f32),
             V((2, rows + 16, LANES), f32), V((2,) + grid, f32),
             V(grid, f32), V(grid, f32), V((2, pad, LANES), f32), V((4, pad, LANES), f32),
             V((2, 2, pad, LANES), f32), V((2, 2, pad, LANES), f32), V((2, 8, LANES), f32), V((2, GROUP, 8, LANES), f32),

time: 21.5 us -> 21.4 us (level)
  no operation moved by 1% of the time
where the time goes in v6:
time: 21.4 us; the launch traced here: 21.3 us
  Pallas kernels  20.5 us (96%)
  local copies, waits for them, and re-layouts  0.82 us (4%)
    pallas_call x1, Pallas kernels, body(): pl.pallas_call(functools.partial(step_kernel, tiles, y_count), out_shape=...  20.5 us
    unnamed x1, local copies, waits for them, and re-layouts  0.82 us

profile of v6, /device:TPU:1, one launch (start us, length us, event | category | flops | bytes accessed | tf_op | source)
XLA Modules:
  0.0 21.3 jit_solution(2874255882923907345)
XLA Ops:
  0.0 20.5 %wave_step.1 = f32[18,64,128]{2,1,0:T(8,128)S(1)} custom-call(f32[18,64,128]{2,1,0:T(8,128)} %bitcast.4, s32[64,128]{1,0:T(8,128)} %bitcast.5, s32[64,256]{1,0:T(8,128)} %mask_hbm.1, s32[64,256]{1,0:T(8,128)} %depth_hbm.1, f32[64,256]{1,0:T(8,128)} %wind_hbm.1, f32[64,256]{1,0:T(8,128)} %angle_hbm.1, f32[8,36]{1,0:T(8,128)} %speed_hbm.1, ...), custom_call_target="tpu_custom_call" | custom-call | tf_op jit(solution)/shard_map/wave_step/pallas_call | solution.py:446
  20.5 0.8 %copy.14 = f32[18,1,8192]{2,1,0:T(1,128)} copy(f32[18,1,8192]{2,1,0:T(1,128)S(1)} %bitcast.3) | data formatting | bytes 1179648

commit v7 on v6

--- a/solution.py
+++ b/solution.py
@@ -43,7 +43,7 @@
     speed_s, friction_s, const_s,
     cos_v, e, order_v, mask_v, depth_v, wind_v, angle_v,
     col_v, water_v, wet_v, inv, nbr, nbr_mask, spd, fri, wx, wy, edge, coef, halo_out, halo_in, rim_out, rim_in, rim_sum, rim_all,
-    part, part_in, total, total_in, damp_out, damp,
+    gain, sent, part, part_in, total, total_in, damp_out, damp,
     ready, passed, in_sem, halo_send, halo_recv, rim_send, rim_recv, r_send, r_recv, a_send, a_recv, b_send, b_recv, c_send, c_recv,
 ):
     comps = e.shape[0]
@@ -122,6 +122,29 @@
             spd[i, inners[n], :] = s[i] * water
             fri[i, at, :] = r[i]
 
+    copies[8].wait()
+    gain[...] = jnp.zeros_like(gain)
+    for a in range(8):
+        for rim_rows in (slice(0, 8), slice(rows + 8, rows + 16)):
+            sent[a, rim_rows, :] = zero8
+
+    def gather_up(step, carry):
+        for pair in range(3):
+            k = 6 * step + 2 * pair
+            d = lax.rem(first + k, ND)
+            i = lax.div(first + k, ND) - f0
+            bx = lax.rem(lax.div(d + 8, 16), 2)
+            by = lax.div(d, 16)
+            cos = [jnp.abs(const_s[d + u]) for u in range(2)]
+            sin = [jnp.abs(const_s[ND + d + u]) for u in range(2)]
+            energy = [e[k + u, inner, :] for u in range(2)]
+            gain[i] += energy[0] + energy[1]
+            gain[2 + 2 * bx + i] += cos[0] * energy[0] + cos[1] * energy[1]
+            gain[6 + 2 * by + i] += sin[0] * energy[0] + sin[1] * energy[1]
+        return carry
+
+    lax.fori_loop(0, comps // 6, gather_up, 0)
+
     narrow = jnp.int16
     lane = lax.broadcasted_iota(jnp.int32, (rows, lanes), 1)
     near = lane.astype(narrow)
@@ -155,7 +178,86 @@
             nbr[2 + b, at, :] = jnp.maximum(found, 0)
             nbr_mask[2 + b, at, :] = jnp.where(inside, water, 0.0)
 
-    copies[8].wait()
+    w0 = const_s[2 * ND + NF + f0]
+    w1 = const_s[2 * ND + NF + f1]
+    v0 = w0 * const_s[2 * ND + f0]
+    v1 = w1 * const_s[2 * ND + f1]
+    for n, at in enumerate(groups):
+        speed = [spd[i, inners[n], :] for i in range(2)]
+        scale = ((w0 * speed[0], w1 * speed[1]), (v0 * speed[0], v1 * speed[1]))
+        water = water_v[at, :]
+        plain = [gain[i, at, :] for i in range(2)]
+        across = [[gain[2 + 2 * a + i, at, :] for i in range(2)] for a in range(4)]
+        for h in range(2):
+            side = [scale[h][0] * across[a][0] + scale[h][1] * across[a][1] for a in range(4)]
+            weights = ((w0, w1), (v0, v1))[h]
+            part[n, h] = water * (weights[0] * plain[0] + weights[1] * plain[1]) - (side[0] + side[1] + side[2] + side[3])
+            for a in range(4):
+                sent[2 * a + h, inners[n], :] = side[a]
+    for n, at in enumerate(groups):
+        for a in range(4):
+            rows_at = slice(8 * n + 7 + 2 * a, 8 * n + 15 + 2 * a) if a < 2 else inners[n]
+            index = nbr[a, at, :]
+            mask = nbr_mask[a, at, :]
+            for h in range(2):
+                part[n, h] += mask * take(sent[2 * a + h, rows_at, :], index)
+    for b, at in ((0, rows - 1), (1, 0)):
+        packed = inv[8 + at : 9 + at, :]
+        back = [(packed & 255) - 1, (packed >> 8) - 1]
+        both = jnp.where(lax.rem(sub, 2) == 0, sent[2 * b, 8 + at : 9 + at, :], sent[2 * b + 1, 8 + at : 9 + at, :])
+        found = jnp.where(sub < 2, back[0], back[1])
+        rim_out[b] = jnp.where(found >= 0, take(both, jnp.maximum(found, 0)), 0.0)
+
+    def halo(b, to):
+        return pltpu.make_async_remote_copy(
+            src_ref=halo_out.at[b], dst_ref=halo_in.at[b], send_sem=halo_send.at[b], recv_sem=halo_recv.at[b],
+            device_id=(to, comp), device_id_type=MESH,
+        )
+
+    def rim(b, n):
+        return pltpu.make_async_remote_copy(
+            src_ref=rim_out.at[b], dst_ref=rim_in.at[b, q], send_sem=rim_send.at[b], recv_sem=rim_recv.at[b],
+            device_id=(beside[b], y * GROUP + n), device_id_type=MESH,
+        )
+
+    def drain(ref, sem):
+        pltpu.make_async_copy(ref, ref, sem).wait()
+
+    def send_beside(b):
+        for n in (3, 4, 2, 5, 1, 6, 0, 7):
+            rim(b, n).start()
+
+    def relay(step):
+        for o in (step + 1, y_count - step - 1):
+            pl.semaphore_signal(passed.at[step], inc=1, device_id=ring[o], device_id_type=MESH)
+
+    def announce():
+        pl.semaphore_wait(barrier, GROUP + 1 + GROUP * lax.div(tile + tiles - 1, tiles))
+
+        relay(0)
+
+        @pl.when(has[1])
+        def _():
+            for n in range(GROUP):
+                pl.semaphore_signal(ready, inc=1, device_id=(beside[1], y * GROUP + n), device_id_type=MESH)
+            send_beside(1)
+
+    announce()
+
+    scatters = {
+        o: pltpu.make_async_remote_copy(
+            src_ref=part.at[lax.rem(q + o, GROUP)], dst_ref=part_in.at[o - 1], send_sem=a_send, recv_sem=a_recv,
+            device_id=group[o], device_id_type=MESH,
+        )
+        for o in order_a
+    }
+    for o in order_a:
+        scatters[o].start()
+
+    pl.semaphore_wait(passed.at[0], 2)
+    if y_count > 4:
+        relay(1)
+
     copies[9].wait()
     pad = edge.shape[1]
     comp_at = first + lax.broadcasted_iota(jnp.int32, (pad, lanes), 0)
@@ -169,74 +271,27 @@
         speed = jnp.where(second, spd[1, 8 + at : 9 + at, :], spd[0, 8 + at : 9 + at, :])
         edge[b, :comps, :] = e[:, 8 + at, :] * speed[:comps]
 
-    w0 = const_s[2 * ND + NF + f0]
-    w1 = const_s[2 * ND + NF + f1]
-    v0 = w0 * const_s[2 * ND + f0]
-    v1 = w1 * const_s[2 * ND + f1]
     for b, at in ((0, rows - 1), (1, 0)):
         packed = inv[8 + at : 9 + at, :]
-        back = [(packed & 255) - 1, (packed >> 8) - 1]
         for h in range(2):
-            found = jnp.broadcast_to(back[h], (pad, lanes))
+            found = jnp.broadcast_to((packed >> 8 if h else packed & 255) - 1, (pad, lanes))
             halo_out[b, h] = jnp.where(found >= 0, take(edge[b], jnp.maximum(found, 0)), 0.0)
-        s0 = jnp.sum((edge[b] * coef[2 * b])[:comps], axis=0, keepdims=True)
-        s1 = jnp.sum((edge[b] * coef[2 * b + 1])[:comps], axis=0, keepdims=True)
-        both = jnp.where(lax.rem(sub, 2) == 0, w0 * s0 + w1 * s1, v0 * s0 + v1 * s1)
-        found = jnp.where(sub < 2, back[0], back[1])
-        rim_out[b] = jnp.where(found >= 0, take(both, jnp.maximum(found, 0)), 0.0)
-
-    def halo(b, to):
-        return pltpu.make_async_remote_copy(
-            src_ref=halo_out.at[b], dst_ref=halo_in.at[b], send_sem=halo_send.at[b], recv_sem=halo_recv.at[b],
-            device_id=(to, comp), device_id_type=MESH,
-        )
-
-    def rim(b, n):
-        return pltpu.make_async_remote_copy(
-            src_ref=rim_out.at[b], dst_ref=rim_in.at[b, q], send_sem=rim_send.at[b], recv_sem=rim_recv.at[b],
-            device_id=(beside[b], y * GROUP + n), device_id_type=MESH,
-        )
-
-    def drain(ref, sem):
-        pltpu.make_async_copy(ref, ref, sem).wait()
-
-    def send_beside(b):
-        for n in (3, 4, 2, 5, 1, 6, 0, 7):
-            rim(b, n).start()
-        halo(b, beside[b]).start()
-
-    def relay(step):
-        for o in (step + 1, y_count - step - 1):
-            pl.semaphore_signal(passed.at[step], inc=1, device_id=ring[o], device_id_type=MESH)
-
-    def announce():
-        pl.semaphore_wait(barrier, GROUP + 1 + GROUP * lax.div(tile + tiles - 1, tiles))
-
-        relay(0)
-
-        @pl.when(has[1])
-        def _():
-            for n in range(GROUP):
-                pl.semaphore_signal(ready, inc=1, device_id=(beside[1], y * GROUP + n), device_id_type=MESH)
-            send_beside(1)
-
-    late = jnp.abs(2 * y - y_count) <= 2
-    pl.when(late)(announce)
+
+    @pl.when(has[1])
+    def _():
+        halo(1, beside[1]).start()
 
     def advect(step, carry):
-        sums = list(carry)
         for pair in range(3):
-            advect_pair(6 * step + 2 * pair, sums)
-        return tuple(sums)
-
-    def advect_pair(k, sums):
+            advect_pair(6 * step + 2 * pair)
+        return carry
+
+    def advect_pair(k):
         f = lax.div(first + k, ND)
         d = lax.rem(first + k, ND)
         i = f - f0
         bx = lax.rem(lax.div(d + 8, 16), 2)
         by = lax.div(d, 16)
-        weight = const_s[2 * ND + NF + f]
-        weight_freq = weight * const_s[2 * ND + f]
         cos = [jnp.abs(const_s[d + u]) for u in range(2)]
         sin = [jnp.abs(const_s[ND + d + u]) for u in range(2)]
         for n, at in enumerate(groups):
@@ -257,30 +312,8 @@
                 moved = energy[u] * water - (cos[u] + sin[u]) * flux[u]
                 moved = moved + cos[u] * (mask_x * gx[u]) + sin[u] * (mask_y * gy[u])
                 p_ref[k + u, at, :] = moved
-                sums[n] = sums[n] + weight * moved
-                sums[GROUP + n] = sums[GROUP + n] + weight_freq * moved
-
-    zero = jnp.zeros((8, lanes), jnp.float32)
-    sums = lax.fori_loop(0, comps // 6, advect, (zero,) * (2 * GROUP))
-    for n in range(GROUP):
-        part[n, 0] = sums[n]
-        part[n, 1] = sums[GROUP + n]
-
-    pl.when(jnp.logical_not(late))(announce)
-
-    scatters = {
-        o: pltpu.make_async_remote_copy(
-            src_ref=part.at[lax.rem(q + o, GROUP)], dst_ref=part_in.at[o - 1], send_sem=a_send, recv_sem=a_recv,
-            device_id=group[o], device_id_type=MESH,
-        )
-        for o in order_a
-    }
-    for o in order_a:
-        scatters[o].start()
-
-    pl.semaphore_wait(passed.at[0], 2)
-    if y_count > 4:
-        relay(1)
+
+    lax.fori_loop(0, comps // 6, advect, 0)
 
     copies[3].wait()
     copies[4].wait()
@@ -316,6 +349,7 @@
     def _():
         pl.semaphore_wait(ready, GROUP)
         send_beside(0)
+        halo(0, beside[0]).start()
 
     for b, at in ((0, 0), (1, rows - 1)):
         @pl.when(has[1 - b])
@@ -458,6 +492,7 @@
             V(grid, f32), V(grid, f32), V((2, pad, LANES), f32), V((4, pad, LANES), f32),
             V((2, 2, pad, LANES), f32), V((2, 2, pad, LANES), f32), V((2, 8, LANES), f32), V((2, GROUP, 8, LANES), f32),
             V((2, 8, LANES), f32), V((y_count - 1, 2, 8, LANES), f32),
+            V((10,) + grid, f32), V((8, rows + 16, LANES), f32),
             V((GROUP, 2, 8, LANES), f32), V((GROUP - 1, 2, 8, LANES), f32),
             V((2, 8, LANES), f32), V((y_count - 1, 2, 8, LANES), f32),
             V((2, 8, LANES), f32), V((GROUP, 2, 8, LANES), f32),

time: 21.4 us -> 20.9 us (0.977)
  Pallas kernels: 20.5 us -> 20 us
    pallas_call x1, Pallas kernels: 20.5 us -> 20 us  [body(): pl.pallas_call(functools.partial(step_kernel, tiles, y_count), out_shape=...]
where the time goes in v7:
time: 20.9 us; the launch traced here: 20.8 us
  Pallas kernels  20 us (96%)
  local copies, waits for them, and re-layouts  0.82 us (4%)
    pallas_call x1, Pallas kernels, body(): pl.pallas_call(functools.partial(step_kernel, tiles, y_count), out_shape=...  20 us
    unnamed x1, local copies, waits for them, and re-layouts  0.82 us

profile of v7, /device:TPU:1, one launch (start us, length us, event | category | flops | bytes accessed | tf_op | source)
XLA Modules:
  0.0 20.8 jit_solution(4401533664724620305)
XLA Ops:
  0.0 20.0 %wave_step.1 = f32[18,64,128]{2,1,0:T(8,128)S(1)} custom-call(f32[18,64,128]{2,1,0:T(8,128)} %bitcast.4, s32[64,128]{1,0:T(8,128)} %bitcast.5, s32[64,256]{1,0:T(8,128)} %mask_hbm.1, s32[64,256]{1,0:T(8,128)} %depth_hbm.1, f32[64,256]{1,0:T(8,128)} %wind_hbm.1, f32[64,256]{1,0:T(8,128)} %angle_hbm.1, f32[8,36]{1,0:T(8,128)} %speed_hbm.1, ...), custom_call_target="tpu_custom_call" | custom-call | tf_op jit(solution)/shard_map/wave_step/pallas_call | solution.py:480
  20.0 0.8 %copy.14 = f32[18,1,8192]{2,1,0:T(1,128)} copy(f32[18,1,8192]{2,1,0:T(1,128)S(1)} %bitcast.3) | data formatting | bytes 1179648

commit v8 on v7

--- a/solution.py
+++ b/solution.py
@@ -143,7 +143,8 @@
             gain[6 + 2 * by + i] += sin[0] * energy[0] + sin[1] * energy[1]
         return carry
 
-    lax.fori_loop(0, comps // 6, gather_up, 0)
+    for step in range(comps // 6):
+        gather_up(step, 0)
 
     narrow = jnp.int16
     lane = lax.broadcasted_iota(jnp.int32, (rows, lanes), 1)
@@ -231,19 +232,8 @@
         for o in (step + 1, y_count - step - 1):
             pl.semaphore_signal(passed.at[step], inc=1, device_id=ring[o], device_id_type=MESH)
 
-    def announce():
-        pl.semaphore_wait(barrier, GROUP + 1 + GROUP * lax.div(tile + tiles - 1, tiles))
-
-        relay(0)
-
-        @pl.when(has[1])
-        def _():
-            for n in range(GROUP):
-                pl.semaphore_signal(ready, inc=1, device_id=(beside[1], y * GROUP + n), device_id_type=MESH)
-            send_beside(1)
-
-    announce()
-
+    pl.semaphore_wait(barrier, GROUP + 1 + GROUP * lax.div(tile + tiles - 1, tiles))
+    relay(0)
     scatters = {
         o: pltpu.make_async_remote_copy(
             src_ref=part.at[lax.rem(q + o, GROUP)], dst_ref=part_in.at[o - 1], send_sem=a_send, recv_sem=a_recv,
@@ -253,6 +243,12 @@
     }
     for o in order_a:
         scatters[o].start()
+
+    @pl.when(has[1])
+    def _():
+        for n in range(GROUP):
+            pl.semaphore_signal(ready, inc=1, device_id=(beside[1], y * GROUP + n), device_id_type=MESH)
+        send_beside(1)
 
     pl.semaphore_wait(passed.at[0], 2)
     if y_count > 4:

time: 20.9 us -> 21.1 us (level)
  no operation moved by 1% of the time
where the time goes in v8:
time: 21.1 us; the launch traced here: 21 us
  Pallas kernels  20.2 us (96%)
  local copies, waits for them, and re-layouts  0.82 us (4%)
    pallas_call x1, Pallas kernels, body(): pl.pallas_call(functools.partial(step_kernel, tiles, y_count), out_shape=...  20.2 us
    unnamed x1, local copies, waits for them, and re-layouts  0.82 us

profile of v8, /device:TPU:1, one launch (start us, length us, event | category | flops | bytes accessed | tf_op | source)
XLA Modules:
  0.0 21.0 jit_solution(956115776969276461)
XLA Ops:
  0.0 20.2 %wave_step.1 = f32[18,64,128]{2,1,0:T(8,128)S(1)} custom-call(f32[18,64,128]{2,1,0:T(8,128)} %bitcast.4, s32[64,128]{1,0:T(8,128)} %bitcast.5, s32[64,256]{1,0:T(8,128)} %mask_hbm.1, s32[64,256]{1,0:T(8,128)} %depth_hbm.1, f32[64,256]{1,0:T(8,128)} %wind_hbm.1, f32[64,256]{1,0:T(8,128)} %angle_hbm.1, f32[8,36]{1,0:T(8,128)} %speed_hbm.1, ...), custom_call_target="tpu_custom_call" | custom-call | tf_op jit(solution)/shard_map/wave_step/pallas_call | solution.py:476
  20.2 0.8 %copy.14 = f32[18,1,8192]{2,1,0:T(1,128)} copy(f32[18,1,8192]{2,1,0:T(1,128)S(1)} %bitcast.3) | data formatting | bytes 1179648
